TPU v7x, 256 devices: a whole 4x4x8 slice. The times are simulated.
256 devices in a mesh: east: 32 (over z, y_hi, core), north: 8 (over x, y_lo).
Axes of the slice: x: 4, y: 4 (y_hi: 2, y_lo: 2; y = y_hi * 2 + y_lo), z: 8, core: 2. Of those that a mesh axis runs over, the one named last changes fastest.
Arguments:
- features: bfloat16 [96, 256, 128, 8], P(None, 'east', 'north'), may hold values from -6 to 6
- brick_active: int32 [32, 16, 1], P('east', 'north'), may hold values 0 or 1
- voxel_occupancy: int32 [256, 128, 8], P('east', 'north'), may hold values 0 or 1
- first_weights: bfloat16 [27, 96, 96], replicated, may hold values from -0.125 to 0.125
- second_weights: bfloat16 [27, 96, 96], replicated, may hold values from -0.125 to 0.125
- head: bfloat16 [13, 96], replicated, may hold values from -0.625 to 0.625
- teacher: bfloat16 [13, 256, 128, 8], P(None, 'east', 'north'), may hold values from -6 to 6
Outputs:
- grad_features: bfloat16 [96, 256, 128, 8], P(None, 'east', 'north')
- grad_first: float32 [27, 96, 96], replicated
- grad_second: float32 [27, 96, 96], replicated
All inputs are finite; a program needn't handle non-finite values. No bound on the sum of `brick_active` or of `voxel_occupancy` on one device may be relied on, other than what follows from the above.
Results may differ from a plain program's by a relative error of at most 0.0058.
Values may be sent and summed in bfloat16 or wider, within the bound.
A program may use at most 128 MiB of HBM per device.

v0:
```python
import math

import jax
import jax.numpy as jnp
from jax import lax
from jax.sharding import PartitionSpec as P


def padded(block, sides, width):
    for axis, dim in sides:
        count = lax.axis_size(axis)
        forward = [(i, i + 1) for i in range(count - 1)]
        backward = [(target, source) for source, target in forward]
        low = lax.ppermute(
            lax.slice_in_dim(block, block.shape[dim] - width, None, axis=dim), axis, forward
        )
        high = lax.ppermute(lax.slice_in_dim(block, 0, width, axis=dim), axis, backward)
        block = jnp.concatenate([low, block, high], axis=dim)
    return block


def offset_of(k):
    return (k // 9 - 1, k // 3 % 3 - 1, k % 3 - 1)


def silu_slope(value):
    sig = jax.nn.sigmoid(value)
    return sig * (1.0 + value * (1.0 - sig))


def stacked(field, sign):
    channels, east, north, plane = field.shape
    wider = padded(field, (("east", 1), ("north", 2)), 1)
    flat = wider.reshape(channels, east + 2, (north + 2) * plane)
    flat = jnp.pad(flat, ((0, 0), (0, 0), (1, 1)))
    pieces = []
    for k in range(27):
        de, dn, du = offset_of(k)
        first = 1 + sign * de
        start = (1 + sign * dn) * plane + sign * du + 1
        pieces.append(flat[:, first : first + east, start : start + north * plane])
    return jnp.stack(pieces, 0).reshape(27 * channels, east * north * plane)


def arrange(part, outputs, channels):
    return part.reshape(outputs, 27, channels).transpose(1, 0, 2)


def per_device(
    features, brick_active, voxel_occupancy, first_weights, second_weights, head, teacher
):
    channels = features.shape[0]
    shape = features.shape[1:]
    east, north, upward = shape
    plane = upward + 2
    wide_shape = (channels, east, north, plane)
    flags = jnp.repeat(brick_active, east // brick_active.shape[0], 0)
    flags = jnp.repeat(flags, north // brick_active.shape[1], 1)
    flags = jnp.repeat(flags, upward // brick_active.shape[2], 2)
    mask = jnp.pad((flags * voxel_occupancy).astype(jnp.float32), ((0, 0), (0, 0), (1, 1)))
    flat_mask = mask.reshape(1, -1)
    wide_features = jnp.pad(features, ((0, 0), (0, 0), (0, 0), (1, 1)))
    a0 = jnp.where(mask[None] > 0, wide_features, jnp.zeros_like(wide_features))
    forward_one = first_weights.transpose(1, 0, 2).reshape(channels, 27 * channels)
    forward_two = second_weights.transpose(1, 0, 2).reshape(channels, 27 * channels)
    backward_one = first_weights.transpose(2, 0, 1).reshape(channels, 27 * channels)
    backward_two = second_weights.transpose(2, 0, 1).reshape(channels, 27 * channels)
    stack_zero = stacked(a0, 1)
    p1 = flat_mask * jnp.dot(forward_one, stack_zero, preferred_element_type=jnp.float32)
    a1 = jax.nn.silu(p1).astype(jnp.bfloat16)
    stack_one = stacked(a1.reshape(wide_shape), 1)
    p2 = flat_mask * jnp.dot(forward_two, stack_one, preferred_element_type=jnp.float32)
    a2 = jax.nn.silu(p2).astype(jnp.bfloat16)
    logits = jnp.dot(head, a2, preferred_element_type=jnp.float32)
    wide_teacher = jnp.pad(teacher, ((0, 0), (0, 0), (0, 0), (1, 1))).reshape(teacher.shape[0], -1)
    g_logits = flat_mask * (logits - wide_teacher.astype(jnp.float32))
    g_a2 = jnp.dot(head.astype(jnp.float32).T, g_logits, precision=lax.Precision.HIGHEST)
    g_p2 = (flat_mask * g_a2 * silu_slope(p2)).astype(jnp.bfloat16)
    total_voxels = lax.axis_size("east") * lax.axis_size("north") * east * north * upward
    scale = 1.0 / math.sqrt(total_voxels)
    contract = (((1,), (1,)), ((), ()))
    second_part = lax.dot_general(g_p2, stack_one, contract, preferred_element_type=jnp.float32)
    second_part = arrange(second_part, channels, channels)
    g_a1 = jnp.dot(
        backward_two, stacked(g_p2.reshape(wide_shape), -1), preferred_element_type=jnp.float32
    )
    g_p1 = (flat_mask * g_a1 * silu_slope(p1)).astype(jnp.bfloat16)
    first_part = lax.dot_general(g_p1, stack_zero, contract, preferred_element_type=jnp.float32)
    first_part = arrange(first_part, channels, channels)
    wide_grad = flat_mask * jnp.dot(
        backward_one, stacked(g_p1.reshape(wide_shape), -1), preferred_element_type=jnp.float32
    )
    grad_features = wide_grad.astype(jnp.bfloat16).reshape(wide_shape)[:, :, :, 1 : plane - 1]
    first_part, second_part = lax.psum((first_part, second_part), ("east", "north"))
    return (grad_features, first_part * scale, second_part * scale)


def solution(mesh):
    in_specs = (
        P(None, "east", "north", None),
        P("east", "north", None),
        P("east", "north", None),
        P(),
        P(),
        P(),
        P(None, "east", "north", None),
    )
    out_specs = (P(None, "east", "north", None), P(), P())
    return jax.shard_map(
        per_device, mesh=mesh, in_specs=in_specs, out_specs=out_specs, check_vma=False
    )
```

profile of v0, /device:TPU:8, one launch (start us, length us, event | category | flops | bytes accessed | tf_op | source)
XLA Modules:
  0.0 724.4 jit_solution(11437631143420705263)
XLA Ops:
  11.6 3.0 collective-permute-start
  15.6 4.1 collective-permute-start.3
  19.7 2.7 collective-permute-start.2
  24.3 2.2 copy.105
  26.7 2.2 copy.108
  32.0 2.6 pad_slice_fusion.6
  55.8 14.9 %copy.104 = bf16[27,96,8,160]{3,2,1,0:T(8,128)(2,1)} copy(bf16[27,96,8,160]{1,3,2,0:T(8,128)(2,1)} %constant_dynamic-update-slice_fusion) | data formatting | bytes 13271040 | tf_op jit(solution)/shard_map/stack | solution.py:42
  70.7 17.5 %reshape.185 = bf16[2592,1280]{1,0:T(8,128)(2,1)} reshape(bf16[27,96,8,160]{3,2,1,0:T(8,128)(2,1)} %copy.104) | data formatting | bytes 13271040 | tf_op jit(solution)/shard_map/reshape | solution.py:42
  88.2 5.2 multiply_convert_fusion.1
  96.1 4.9 collective-permute-start.4
  102.7 1.8 copy.116
  109.8 1.8 copy.119
  118.9 1.8 copy.124
  120.8 1.9 copy.125
  124.5 1.8 copy.127
  131.8 1.8 copy.131
  133.6 1.8 copy.132
  175.5 1.9 collective-permute-start.7
  177.5 4.8 collective-permute-start.6
  186.9 2.6 pad_slice_fusion
  210.8 14.9 %copy.107 = bf16[27,96,8,160]{3,2,1,0:T(8,128)(2,1)} copy(bf16[27,96,8,160]{1,3,2,0:T(8,128)(2,1)} %constant_dynamic-update-slice_fusion.30) | data formatting | bytes 13271040 | tf_op jit(solution)/shard_map/stack | solution.py:42
  225.6 17.5 %reshape.189 = bf16[2592,1280]{1,0:T(8,128)(2,1)} reshape(bf16[27,96,8,160]{3,2,1,0:T(8,128)(2,1)} %copy.107) | data formatting | bytes 13271040 | tf_op jit(solution)/shard_map/reshape | solution.py:42
  243.2 4.3 fusion.3
  251.6 5.8 collective-permute-start.8
  267.9 1.8 copy.147
  271.6 1.8 copy.149
  275.2 1.9 copy.151
  277.1 1.8 copy.152
  278.9 1.8 copy.153
  280.8 1.8 copy.154
  282.6 1.8 copy.155
  288.1 1.9 copy.158
  331.8 1.9 collective-permute-start.11
  333.7 4.8 collective-permute-start.10
  362.8 14.9 %copy.112 = bf16[27,96,8,160]{3,2,1,0:T(8,128)(2,1)} copy(bf16[27,96,8,160]{1,3,2,0:T(8,128)(2,1)} %constant_dynamic-update-slice_fusion.60) | data formatting | bytes 13271040 | tf_op jit(solution)/shard_map/stack | solution.py:42
  377.6 17.6 %reshape.193 = bf16[2592,1280]{1,0:T(8,128)(2,1)} reshape(bf16[27,96,8,160]{3,2,1,0:T(8,128)(2,1)} %copy.112) | data formatting | bytes 13271040 | tf_op jit(solution)/shard_map/reshape | solution.py:42
  395.3 4.3 fusion.6
  400.0 6.5 collective-permute-start.12
  406.5 6.5 convolution_bitcast_fusion.1
  414.6 4.9 collective-permute-done.13
  419.5 1.9 collective-permute-start.15
  421.4 5.9 collective-permute-start.14
  427.3 6.4 convolution_bitcast_fusion.2
  456.4 14.9 %copy.114 = bf16[27,96,8,160]{3,2,1,0:T(8,128)(2,1)} copy(bf16[27,96,8,160]{1,3,2,0:T(8,128)(2,1)} %constant_dynamic-update-slice_fusion.90) | data formatting | bytes 13271040 | tf_op jit(solution)/shard_map/stack | solution.py:42
  471.3 17.6 %reshape.197 = bf16[2592,1280]{1,0:T(8,128)(2,1)} reshape(bf16[27,96,8,160]{3,2,1,0:T(8,128)(2,1)} %copy.114) | data formatting | bytes 13271040 | tf_op jit(solution)/shard_map/reshape | solution.py:42
  489.0 4.2 fusion.9
  494.4 219.6 %all-reduce.10.cloned.1.call-done = (f32[27,96,96]{2,1,0:T(8,128)}, f32[27,96,96]{2,1,0:T(8,128)}) async-done(((f32[27,96,96]{2,1,0:T(8,128)}, f32[27,96,96]{2,1,0:T(8,128)}), (f32[27,96,96]{2,1,0:T(8,128)}, f32[27,96,96]{2,1,0:T(8,128)})) %all-reduce.10.cloned.1.call-update) | async-done | bytes 1990672 | tf_op jit(solution)/shard_map/psum | solution.py:94
  713.9 3.4 broadcast_multiply_fusion
  (289 shorter events, 235.4 us)
Async XLA Ops:
  7.2 240.3 %copy-start = (bf16[13,96]{1,0:T(8,128)(2,1)S(1)}, bf16[13,96]{1,0:T(8,128)(2,1)}, u32[]{:S(2)}) copy-start(bf16[13,96]{1,0:T(8,128)(2,1)} %param.12) | copy-start | bytes 7492
  7.2 706.8 %all-reduce.10.cloned.1.call-start = ((), (), s32[]{:S(2)}) async-start(), calls=%async_computation | async-start | bytes 5308416 | tf_op jit(solution)/shard_map/psum | solution.py:94
  10.3 5.3 collective-permute-start.1
  11.6 4.0 collective-permute-start
  15.6 13.2 %collective-permute-start.3 = (bf16[96,10,1,10]{0,3,2,1:T(8,128)(2,1)S(1)}, bf16[96,10,1,10]{0,3,2,1:T(8,128)(2,1)S(1)}, u32[]{:S(2)}, u32[]{:S(2)}) collective-permute-start(bf16[96,10,1,10]{0,3,2,1:T(8,128)(2,1)S(1)} %get-tuple-element.12), channel_id=1, source_target_pairs={{1,0},{2,1},{3,2},{4,3},{5,4},{6,5},{7,6},{9,8},{10,9},{11,10},{12... | collective-permute-start | bytes 57608 | tf_op jit(solution)/shard_map/ppermute | solution.py:17
  19.7 9.2 %collective-permute-start.2 = (bf16[96,10,1,10]{0,3,2,1:T(8,128)(2,1)S(1)}, bf16[96,10,1,10]{0,3,2,1:T(8,128)(2,1)S(1)}, u32[]{:S(2)}, u32[]{:S(2)}) collective-permute-start(bf16[96,10,1,10]{0,3,2,1:T(8,128)(2,1)S(1)} %get-tuple-element.11), channel_id=1, source_target_pairs={{0,1},{1,2},{2,3},{3,4},{4,5},{5,6},{6,7},{8,9},{9,10},{10,11},{11... | collective-permute-start | bytes 57608 | tf_op jit(solution)/shard_map/ppermute | solution.py:14
  96.1 78.5 %collective-permute-start.4 = (bf16[96,1,16,10]{0,3,2,1:T(8,128)(2,1)}, bf16[96,1,16,10]{0,3,2,1:T(8,128)(2,1)}, u32[]{:S(2)}, u32[]{:S(2)}) collective-permute-start(bf16[96,1,16,10]{0,3,2,1:T(8,128)(2,1)} %get-tuple-element.18), channel_id=1, source_target_pairs={{0,8},{8,16},{16,24},{24,32},{32,40},{40,48},{48,56},{56,64},{64,7... | collective-permute-start | bytes 92168 | tf_op jit(solution)/shard_map/ppermute | solution.py:14
  100.9 74.6 %collective-permute-start.5 = (bf16[96,1,16,10]{0,3,2,1:T(8,128)(2,1)}, bf16[96,1,16,10]{0,3,2,1:T(8,128)(2,1)S(1)}, u32[]{:S(2)}, u32[]{:S(2)}) collective-permute-start(bf16[96,1,16,10]{0,3,2,1:T(8,128)(2,1)} %get-tuple-element.17), channel_id=1, source_target_pairs={{8,0},{16,8},{24,16},{32,24},{40,32},{48,40},{56,48},{64,56},{72,6... | collective-permute-start | bytes 92168 | tf_op jit(solution)/shard_map/ppermute | solution.py:17
  175.5 7.5 %collective-permute-start.7 = (bf16[96,10,1,10]{0,3,2,1:T(8,128)(2,1)S(1)}, bf16[96,10,1,10]{0,3,2,1:T(8,128)(2,1)S(1)}, u32[]{:S(2)}, u32[]{:S(2)}) collective-permute-start(bf16[96,10,1,10]{0,3,2,1:T(8,128)(2,1)S(1)} %get-tuple-element.10), channel_id=1, source_target_pairs={{1,0},{2,1},{3,2},{4,3},{5,4},{6,5},{7,6},{9,8},{10,9},{11,10},{12... | collective-permute-start | bytes 57608 | tf_op jit(solution)/shard_map/ppermute | solution.py:17
  177.5 6.5 collective-permute-start.6
  243.2 4.3 copy-start.6
  248.3 0.7 copy-start.2
  251.6 79.2 %collective-permute-start.8 = (bf16[96,1,16,10]{0,3,2,1:T(8,128)(2,1)}, bf16[96,1,16,10]{0,3,2,1:T(8,128)(2,1)}, u32[]{:S(2)}, u32[]{:S(2)}) collective-permute-start(bf16[96,1,16,10]{0,3,2,1:T(8,128)(2,1)} %get-tuple-element.16), channel_id=1, source_target_pairs={{0,8},{8,16},{16,24},{24,32},{32,40},{40,48},{48,56},{56,64},{64,7... | collective-permute-start | bytes 92168 | tf_op jit(solution)/shard_map/ppermute | solution.py:14
  257.5 74.3 %collective-permute-start.9 = (bf16[96,1,16,10]{0,3,2,1:T(8,128)(2,1)}, bf16[96,1,16,10]{0,3,2,1:T(8,128)(2,1)S(1)}, u32[]{:S(2)}, u32[]{:S(2)}) collective-permute-start(bf16[96,1,16,10]{0,3,2,1:T(8,128)(2,1)} %get-tuple-element.15), channel_id=1, source_target_pairs={{8,0},{16,8},{24,16},{32,24},{40,32},{48,40},{56,48},{64,56},{72,6... | collective-permute-start | bytes 92168 | tf_op jit(solution)/shard_map/ppermute | solution.py:17
  331.8 7.5 %collective-permute-start.11 = (bf16[96,10,1,10]{0,3,2,1:T(8,128)(2,1)S(1)}, bf16[96,10,1,10]{0,3,2,1:T(8,128)(2,1)S(1)}, u32[]{:S(2)}, u32[]{:S(2)}) collective-permute-start(bf16[96,10,1,10]{0,3,2,1:T(8,128)(2,1)S(1)} %get-tuple-element.8), channel_id=1, source_target_pairs={{1,0},{2,1},{3,2},{4,3},{5,4},{6,5},{7,6},{9,8},{10,9},{11,10},{12... | collective-permute-start | bytes 57608 | tf_op jit(solution)/shard_map/ppermute | solution.py:17
  333.7 6.5 collective-permute-start.10
  377.6 17.6 %copy-start.4 = (bf16[27,96,96]{2,1,0:T(8,128)(2,1)S(1)}, bf16[27,96,96]{2,1,0:T(8,128)(2,1)}, u32[]{:S(2)}) copy-start(bf16[27,96,96]{2,1,0:T(8,128)(2,1)} %param.11) | copy-start | bytes 1492996
  377.6 17.6 %copy-start.7 = (f32[96,1280]{1,0:T(8,128)S(1)}, f32[96,1280]{1,0:T(8,128)}, u32[]{:S(2)}) copy-start(f32[96,1280]{1,0:T(8,128)} %get-tuple-element.76) | copy-start | bytes 1474564
  395.3 11.2 %copy-start.3 = (bf16[96,1280]{1,0:T(8,128)(2,1)S(1)}, bf16[96,1280]{1,0:T(8,128)(2,1)}, u32[]{:S(2)}) copy-start(bf16[96,1280]{1,0:T(8,128)(2,1)} %copy-done.2) | copy-start | bytes 737284
  400.0 14.5 %collective-permute-start.12 = (bf16[96,1,16,10]{0,3,2,1:T(8,128)(2,1)S(1)}, bf16[96,1,16,10]{0,3,2,1:T(8,128)(2,1)S(1)}, u32[]{:S(2)}, u32[]{:S(2)}) collective-permute-start(bf16[96,1,16,10]{0,3,2,1:T(8,128)(2,1)S(1)} %get-tuple-element.14), channel_id=1, source_target_pairs={{0,8},{8,16},{16,24},{24,32},{32,40},{40,48},{48,56},{56,64},{64,7... | collective-permute-start | bytes 92168 | tf_op jit(solution)/shard_map/ppermute | solution.py:14
  413.0 6.5 collective-permute-start.13
  419.5 14.3 %collective-permute-start.15 = (bf16[96,10,1,10]{0,3,2,1:T(8,128)(2,1)S(1)}, bf16[96,10,1,10]{0,3,2,1:T(8,128)(2,1)S(1)}, u32[]{:S(2)}, u32[]{:S(2)}) collective-permute-start(bf16[96,10,1,10]{0,3,2,1:T(8,128)(2,1)S(1)} %get-tuple-element.6), channel_id=1, source_target_pairs={{1,0},{2,1},{3,2},{4,3},{5,4},{6,5},{7,6},{9,8},{10,9},{11,10},{12... | collective-permute-start | bytes 57608 | tf_op jit(solution)/shard_map/ppermute | solution.py:17
  421.4 12.4 %collective-permute-start.14 = (bf16[96,10,1,10]{0,3,2,1:T(8,128)(2,1)S(1)}, bf16[96,10,1,10]{0,3,2,1:T(8,128)(2,1)S(1)}, u32[]{:S(2)}, u32[]{:S(2)}) collective-permute-start(bf16[96,10,1,10]{0,3,2,1:T(8,128)(2,1)S(1)} %get-tuple-element.5), channel_id=1, source_target_pairs={{0,1},{1,2},{2,3},{3,4},{4,5},{5,6},{6,7},{8,9},{9,10},{10,11},{11... | collective-permute-start | bytes 57608 | tf_op jit(solution)/shard_map/ppermute | solution.py:14
  471.3 17.7 %copy-start.5 = (bf16[27,96,96]{2,1,0:T(8,128)(2,1)S(1)}, bf16[27,96,96]{2,1,0:T(8,128)(2,1)}, u32[]{:S(2)}) copy-start(bf16[27,96,96]{2,1,0:T(8,128)(2,1)} %param.10) | copy-start | bytes 1492996
  471.3 246.1 %copy-start.1 = (bf16[13,96]{1,0:T(8,128)(2,1)S(1)}, bf16[13,96]{1,0:T(8,128)(2,1)}, u32[]{:S(2)}) copy-start(bf16[13,96]{1,0:T(8,128)(2,1)} %param.12) | copy-start | bytes 7492
Sparse Core Ops, SparseCore 0:
  433.9 280.0 all-reduce.9
where the time goes:
time: 738 us; the launch traced here: 724 us
  local copies, waits for them, and re-layouts  391 us (53%)
  waiting for transfers between devices  226 us (31%)
  starting transfers between devices  54.3 us (7%)
  matrix products  31.7 us (4%)
  between operations  14.9 us (2%)
    psum x1, waiting for transfers between devices, per_device(): lax.psum((first_part, second_part), ('east', 'north'))  220 us
    unnamed x180, local copies, waits for them, and re-layouts  162 us
    another operation x64, local copies, waits for them, and re-layouts, stacked(): return jnp.stack(pieces, 0).reshape(27 * channels, east * north * plane)  135 us
    reshape x4, local copies, waits for them, and re-layouts, stacked(): return jnp.stack(pieces, 0).reshape(27 * channels, east * north * plane)  70.4 us
    ppermute x8, starting transfers between devices, padded(): lax.ppermute(lax.slice_in_dim(block, block.shape[dim] - width, None, axis...  38.5 us
    ppermute x8, starting transfers between devices, padded(): lax.ppermute(lax.slice_in_dim(block, 0, width, axis=dim), axis, backward)  15.8 us
  transfers between devices with their start and end apart: 17, of which 4 were waited for; matrix products, arithmetic and copies ran while one was open for 31% of the time, Pallas kernels for 0%

commit v1 on v0

v1 whole, which is shorter than its diff:
```python
import functools
import math

import jax
import jax.numpy as jnp
from jax import lax
from jax.experimental import pallas as pl
from jax.experimental.pallas import tpu as pltpu
from jax.sharding import PartitionSpec as P

MESH = pl.DeviceIdType.MESH
VM = pltpu.VMEM
F32 = jnp.float32
BF = jnp.bfloat16
SIDES = tuple((a, b) for a in (-1, 0, 1) for b in (-1, 0, 1) if (a, b) != (0, 0))
NT = (((1,), (1,)), ((), ()))


def part(side, size):
    if side > 0:
        return size - 2, 2, 0
    if side < 0:
        return 0, 2, size + 2
    return 0, size, 2


def exchange_start(x_ref, ext_ref, send, recv, local):
    east, north = lax.axis_size("east"), lax.axis_size("north")
    e, n = lax.axis_index("east"), lax.axis_index("north")
    size_e, size_n = x_ref.shape[0], x_ref.shape[1] // 8
    barrier = pltpu.get_barrier_semaphore()

    def peer(side):
        return (lax.rem(e + side[0] + east, east), lax.rem(n + side[1] + north, north))

    for side in SIDES:
        pl.semaphore_signal(barrier, inc=1, device_id=peer(side), device_id_type=MESH)
    centre = pltpu.make_async_copy(
        x_ref, ext_ref.at[pl.ds(2, size_e), pl.ds(16, size_n * 8)], local
    )
    centre.start()
    pl.semaphore_wait(barrier, len(SIDES))
    copies = [centre]
    for i, side in enumerate(SIDES):
        se, le, de = part(side[0], size_e)
        sn, ln, dn = part(side[1], size_n)
        copy = pltpu.make_async_remote_copy(
            src_ref=x_ref.at[pl.ds(se, le), pl.ds(sn * 8, ln * 8)],
            dst_ref=ext_ref.at[pl.ds(de, le), pl.ds(dn * 8, ln * 8)],
            send_sem=send.at[i],
            recv_sem=recv.at[i],
            device_id=peer(side),
            device_id_type=MESH,
        )
        copy.start()
        copies.append(copy)
    return copies


def exchange_end(copies, ext_ref):
    for copy in copies:
        copy.wait()
    e, n = lax.axis_index("east"), lax.axis_index("north")
    wide_e, wide_n, lanes = ext_ref.shape

    @pl.when(e == 0)
    def _():
        ext_ref[0:2] = jnp.zeros((2, wide_n, lanes), ext_ref.dtype)

    @pl.when(e == lax.axis_size("east") - 1)
    def _():
        ext_ref[wide_e - 2 : wide_e] = jnp.zeros((2, wide_n, lanes), ext_ref.dtype)

    @pl.when(n == 0)
    def _():
        ext_ref[:, 0:16] = jnp.zeros((wide_e, 16, lanes), ext_ref.dtype)

    @pl.when(n == lax.axis_size("north") - 1)
    def _():
        ext_ref[:, wide_n - 16 : wide_n] = jnp.zeros((wide_e, 16, lanes), ext_ref.dtype)


def build(src_ref, first, planes, start, count, out_ref):
    wide = src_ref.shape[1] // 8
    up = lax.broadcasted_iota(jnp.int32, (wide, 8, 128), 1)

    def body(i, carry):
        x = src_ref[first + i].astype(F32).reshape(wide, 8, 128)
        below = jnp.where(up == 0, 0.0, pltpu.roll(x, 1, 1))
        above = jnp.where(up == 7, 0.0, pltpu.roll(x, 7, 1))
        rows = pl.ds(pl.multiple_of(i * (count * 8), 16), count * 8)
        for dn in range(3):
            for du, piece in enumerate((below, x, above)):
                block = (dn * 3 + du) * 128
                y = piece[start + dn : start + dn + count].reshape(count * 8, 128)
                out_ref[rows, block : block + 128] = y.astype(BF)
        return carry

    lax.fori_loop(0, planes, body, 0)


def lay_forward(w_ref, out_ref):
    out_ref[...] = jnp.zeros_like(out_ref)
    size = w_ref.shape[1]
    for k in range(27):
        out_ref[k // 9, 0:size, (k % 9) * 128 : (k % 9) * 128 + size] = w_ref[k]


def lay_backward(w_ref, out_ref):
    out_ref[...] = jnp.zeros_like(out_ref)
    size = w_ref.shape[1]
    for k in range(27):
        out_ref[k // 9, (k % 9) * 128 : (k % 9) * 128 + size, 0:size] = w_ref[26 - k]


def convolve(x_ref, plane, rows, w_ref, acc_ref, transposed):
    acc_ref[0:rows] = jnp.zeros((rows, 128), F32)

    def body(i, carry):
        x = x_ref[pl.ds(pl.multiple_of(i * plane, 16), rows)]
        if transposed:
            y = lax.dot_general(x, w_ref[i], NT, preferred_element_type=F32)
        else:
            y = jnp.dot(x, w_ref[i], preferred_element_type=F32)
        acc_ref[0:rows] += y
        return carry

    lax.fori_loop(0, 3, body, 0)


def weight_grad(g_ref, x_ref, plane, out_ref):
    size = out_ref.shape[1]

    def body(i, carry):
        x = x_ref[pl.ds(pl.multiple_of(i * plane, 16), g_ref.shape[1])]
        y = jnp.dot(g_ref[...], x, preferred_element_type=F32)
        for b in range(9):
            out_ref[i * 9 + b] = y[0:size, b * 128 : b * 128 + size]
        return carry

    lax.fori_loop(0, 3, body, 0)


def slope_of(value, sig):
    return sig * (1.0 + value * (1.0 - sig))


def forward_kernel(
    x_ref, w1_ref, w2_ref, head_ref, teacher_ref,
    g2_ref, ext_out, slope_out, grad_ref,
    ext_ref, wf1, wf2, cols1, cols2, acc, a1_ref, gt_ref,
    send, recv, local,
):
    copies = exchange_start(x_ref, ext_ref, send, recv, local)
    lay_forward(w1_ref, wf1)
    lay_forward(w2_ref, wf2)
    exchange_end(copies, ext_ref)
    size_e, rows = x_ref.shape[0], x_ref.shape[1]
    north = rows // 8
    wide = rows + 16
    channels = w1_ref.shape[1]
    ext_out[...] = ext_ref[...]
    build(ext_ref, 0, size_e + 4, 0, north + 2, cols1)
    convolve(cols1, wide, (size_e + 2) * wide, wf1, acc, True)

    def first(i, carry):
        at = pl.ds(pl.multiple_of(i * wide, 16), wide)
        x = ext_ref[i + 1].astype(F32)[8 : 8 + wide]
        mask = jnp.broadcast_to(x[:, channels : channels + 1], (wide, 128))
        p1 = mask * acc[at]
        sig = jax.nn.sigmoid(p1)
        a1_ref[i] = (p1 * sig).astype(BF)
        slope_out[at] = mask * slope_of(p1, sig)
        return carry

    lax.fori_loop(0, size_e + 2, first, 0)
    build(a1_ref, 0, size_e + 2, 0, north, cols2)
    convolve(cols2, rows, size_e * rows, wf2, acc, True)
    head = head_ref[...]

    def second(i, carry):
        at = pl.ds(pl.multiple_of(i * rows, 16), rows)
        x = ext_ref[i + 2, 16 : 16 + rows].astype(F32)
        mask = jnp.broadcast_to(x[:, channels : channels + 1], (rows, 128))
        p2 = mask * acc[at]
        sig = jax.nn.sigmoid(p2)
        a2 = (p2 * sig).astype(BF)
        logits = lax.dot_general(a2, head, NT, preferred_element_type=F32)
        g = mask * (logits - teacher_ref[i].astype(F32))
        high = g.astype(BF)
        rest = g - high.astype(F32)
        mid = rest.astype(BF)
        low = (rest - mid.astype(F32)).astype(BF)
        back = jnp.dot(low, head, preferred_element_type=F32)
        back = back + jnp.dot(mid, head, preferred_element_type=F32)
        back = back + jnp.dot(high, head, preferred_element_type=F32)
        g2 = (mask * back * slope_of(p2, sig)).astype(BF)
        g2_ref[i] = g2
        gt_ref[:, at] = g2.astype(F32).T.astype(BF)
        return carry

    lax.fori_loop(0, size_e, second, 0)
    weight_grad(gt_ref, cols2, rows, grad_ref)


def backward_kernel(
    g2_ref, w1_ref, w2_ref, ext0_ref, slope_ref,
    out_ref, grad_ref,
    ext_ref, wb1, wb2, cols0, cols1, cols2, acc, g1_ref, gt_ref,
    send, recv, local,
):
    copies = exchange_start(g2_ref, ext_ref, send, recv, local)
    size_e, rows = g2_ref.shape[0], g2_ref.shape[1]
    north = rows // 8
    wide = rows + 16
    channels = w1_ref.shape[1]
    lay_backward(w1_ref, wb1)
    lay_backward(w2_ref, wb2)
    build(ext0_ref, 1, size_e + 2, 1, north, cols0)
    exchange_end(copies, ext_ref)
    build(ext_ref, 0, size_e + 4, 0, north + 2, cols1)
    convolve(cols1, wide, (size_e + 2) * wide, wb2, acc, False)

    def first(i, carry):
        at = pl.ds(pl.multiple_of(i * wide, 16), wide)
        g1_ref[i] = (acc[at] * slope_ref[at]).astype(BF)
        return carry

    lax.fori_loop(0, size_e + 2, first, 0)

    def turn(i, carry):
        at = pl.ds(pl.multiple_of(i * rows, 16), rows)
        gt_ref[:, at] = g1_ref[i + 1].astype(F32)[8 : 8 + rows].T.astype(BF)
        return carry

    lax.fori_loop(0, size_e, turn, 0)
    weight_grad(gt_ref, cols0, rows, grad_ref)
    build(g1_ref, 0, size_e + 2, 0, north, cols2)
    convolve(cols2, rows, size_e * rows, wb1, acc, False)

    def last(i, carry):
        at = pl.ds(pl.multiple_of(i * rows, 16), rows)
        x = ext0_ref[i + 2, 16 : 16 + rows].astype(F32)
        mask = jnp.broadcast_to(x[:, channels : channels + 1], (rows, 128))
        out_ref[i] = (mask * acc[at])[:, 0:channels].astype(BF)
        return carry

    lax.fori_loop(0, size_e, last, 0)


def call(kernel, ident, outs, scratch, *args):
    return pl.pallas_call(
        kernel,
        out_shape=outs,
        in_specs=[pl.BlockSpec(memory_space=VM)] * len(args),
        out_specs=[pl.BlockSpec(memory_space=VM)] * len(outs),
        scratch_shapes=scratch,
        compiler_params=pltpu.CompilerParams(
            collective_id=ident, has_side_effects=True, vmem_limit_bytes=60 << 20
        ),
    )(*args)


def per_device(
    features, brick_active, voxel_occupancy, first_weights, second_weights, head, teacher
):
    channels, east, north, upward = features.shape
    classes = head.shape[0]
    rows = north * upward
    flags = jnp.repeat(brick_active, east // brick_active.shape[0], 0)
    flags = jnp.repeat(flags, north // brick_active.shape[1], 1)
    flags = jnp.repeat(flags, upward // brick_active.shape[2], 2)
    mask = (flags * voxel_occupancy)[..., None]
    a0 = features.transpose(1, 2, 3, 0)
    a0 = jnp.where(mask > 0, a0, jnp.zeros_like(a0))
    a0 = jnp.pad(a0, ((0, 0), (0, 0), (0, 0), (0, 128 - channels)))
    lane = lax.broadcasted_iota(jnp.int32, (1, 1, 1, 128), 3)
    x0 = jnp.where(lane == channels, mask.astype(BF), a0).reshape(east, rows, 128)
    wide_teacher = jnp.pad(teacher.transpose(1, 2, 3, 0), ((0, 0), (0, 0), (0, 0), (0, 128 - classes)))
    wide_teacher = wide_teacher.reshape(east, rows, 128)
    wide_head = jnp.pad(head, ((0, 128 - classes), (0, 128 - channels)))
    shape = jax.ShapeDtypeStruct
    sems = [pltpu.SemaphoreType.DMA((8,)), pltpu.SemaphoreType.DMA((8,)), pltpu.SemaphoreType.DMA]
    big = (east + 2) * (rows + 16)
    ext = (east + 4, rows + 32, 128)
    grad = shape((27, channels, channels), F32)
    g2, ext0, slope, second_part = call(
        forward_kernel,
        1,
        (shape((east, rows, 128), BF), shape(ext, BF), shape((big, 128), F32), grad),
        [
            VM(ext, BF),
            VM((3, 128, 1152), BF),
            VM((3, 128, 1152), BF),
            VM(((east + 4) * (rows + 16), 1152), BF),
            VM(((east + 2) * rows, 1152), BF),
            VM((big, 128), F32),
            VM((east + 2, rows + 16, 128), BF),
            VM((128, east * rows), BF),
        ]
        + sems,
        x0,
        first_weights,
        second_weights,
        wide_head,
        wide_teacher,
    )
    out, first_part = call(
        backward_kernel,
        2,
        (shape((east, rows, channels), BF), grad),
        [
            VM(ext, BF),
            VM((3, 1152, 128), BF),
            VM((3, 1152, 128), BF),
            VM(((east + 2) * rows, 1152), BF),
            VM(((east + 4) * (rows + 16), 1152), BF),
            VM(((east + 2) * rows, 1152), BF),
            VM((big, 128), F32),
            VM((east + 2, rows + 16, 128), BF),
            VM((128, east * rows), BF),
        ]
        + sems,
        g2,
        first_weights,
        second_weights,
        ext0,
        slope,
    )
    grad_features = out.reshape(east, north, upward, channels).transpose(3, 0, 1, 2)
    total_voxels = lax.axis_size("east") * lax.axis_size("north") * east * north * upward
    scale = 1.0 / math.sqrt(total_voxels)
    first_part, second_part = lax.psum((first_part, second_part), ("east", "north"))
    return (grad_features, first_part * scale, second_part * scale)


def solution(mesh):
    in_specs = (
        P(None, "east", "north", None),
        P("east", "north", None),
        P("east", "north", None),
        P(),
        P(),
        P(),
        P(None, "east", "north", None),
    )
    out_specs = (P(None, "east", "north", None), P(), P())
    return jax.shard_map(
        per_device, mesh=mesh, in_specs=in_specs, out_specs=out_specs, check_vma=False
    )
```

time: 738 us -> 339 us (0.46)
  the two profiles are of different devices: /device:TPU:8 before, /device:TPU:1 now
where the time goes in v1:
time: 339 us; the launch traced here: 337 us
  waiting for transfers between devices  260 us (77%)
  Pallas kernels  51 us (15%)
  between operations  14.1 us (4%)
  other arithmetic  7.43 us (2%)
  local copies, waits for them, and re-layouts  4.44 us (1%)
    psum x1, waiting for transfers between devices, per_device(): lax.psum((first_part, second_part), ('east', 'north'))  260 us
    pallas_call x2, Pallas kernels, call(): pl.pallas_call(kernel, out_shape=outs, in_specs=[pl.BlockSpec(memory_spac...  51 us
  transfers between devices with their start and end apart: 1, of which 1 were waited for; matrix products, arithmetic and copies ran while one was open for 0% of the time, Pallas kernels for 0%

profile of v1, /device:TPU:1, one launch (start us, length us, event | category | flops | bytes accessed | tf_op | source)
XLA Modules:
  0.0 336.8 jit_solution(4626159033764770712)
XLA Ops:
  7.2 0.0 all-reduce.6.cloned.1.call-start
  7.2 0.7 broadcast_in_dim.36
  7.9 0.1 broadcast_in_dim.37
  8.0 0.8 multiply_compare_fusion
  8.8 0.8 multiply_convert_fusion
  9.6 0.1 copy.11
  9.7 0.1 copy.10
  9.8 1.4 copy.13
  11.2 1.3 pad.13.head_ref
  12.5 1.1 select_bitcast_fusion.1
  13.7 1.0 pad_bitcast_fusion
  14.7 29.4 %shard_map.97 = (bf16[8,128,128]{2,1,0:T(8,128)(2,1)}, bf16[12,160,128]{2,1,0:T(8,128)(2,1)}, f32[1440,128]{1,0:T(8,128)}, f32[27,96,96]{2,1,0:T(8,128)}) custom-call(bf16[8,128,128]{2,1,0:T(8,128)(2,1)} %get-tuple-element.18.x_ref, bf16[27,96,96]{2,1,0:T(8,128)(2,1)} %w1_ref.3, bf16[27,96,96]{2,1,0:T(8,128)(2,1)} %w2_ref.3, bf16[128,128]{1,0:T(8,128)(2,1)} %pad.13.head_ref, ...), custom_call_target="tpu_custom_call" | custom-call | tf_op jit(solution)/shard_map/pallas_call | solution.py:252
  44.1 21.6 %shard_map.98 = (bf16[8,128,96]{2,1,0:T(8,128)(2,1)}, f32[27,96,96]{2,1,0:T(8,128)}) custom-call(bf16[8,128,128]{2,1,0:T(8,128)(2,1)} %get-tuple-element.9.g2_ref, bf16[27,96,96]{2,1,0:T(8,128)(2,1)} %w1_ref.3, bf16[27,96,96]{2,1,0:T(8,128)(2,1)} %w2_ref.3, bf16[12,160,128]{2,1,0:T(8,128)(2,1)} %get-tuple-element.10.ext0_ref, ...), custom_call_target="tpu_custom_call" | custom-call | tf_op jit(solution)/shard_map/pallas_call | solution.py:252
  65.7 0.0 all-reduce.6.cloned.1.call-update
  65.7 259.8 %all-reduce.6.cloned.1.call-done = (f32[27,96,96]{2,1,0:T(8,128)}, f32[27,96,96]{2,1,0:T(8,128)}) async-done(((f32[27,96,96]{2,1,0:T(8,128)}, f32[27,96,96]{2,1,0:T(8,128)}), (f32[27,96,96]{2,1,0:T(8,128)}, f32[27,96,96]{2,1,0:T(8,128)})) %all-reduce.6.cloned.1.call-update) | async-done | bytes 1990672 | tf_op jit(solution)/shard_map/psum | solution.py:333
  325.5 0.0 copy-start
  325.5 2.6 broadcast_multiply_fusion.1
  328.1 0.0 copy-done
  328.1 0.0 copy-start.1
  328.1 1.2 broadcast_multiply_fusion
  329.3 0.0 copy-done.1
  329.3 0.7 copy.17
  (1 shorter events, 0.0 us)
Async XLA Ops:
  7.2 318.4 %all-reduce.6.cloned.1.call-start = ((), (), s32[]{:S(2)}) async-start(), calls=%async_computation | async-start | bytes 5308416 | tf_op jit(solution)/shard_map/psum | solution.py:333
  325.5 2.6 copy-start
  328.1 1.2 copy-start.1
Sparse Core Ops, SparseCore 0:
  65.9 259.6 all-reduce.5

commit v2 on v1

--- a/solution.py
+++ b/solution.py
@@ -24,7 +24,7 @@
     return 0, size, 2
 
 
-def exchange_start(x_ref, ext_ref, send, recv, local):
+def exchange_start(x_ref, ext_ref, send, recv, local, others=()):
     east, north = lax.axis_size("east"), lax.axis_size("north")
     e, n = lax.axis_index("east"), lax.axis_index("north")
     size_e, size_n = x_ref.shape[0], x_ref.shape[1] // 8
@@ -33,13 +33,13 @@
     def peer(side):
         return (lax.rem(e + side[0] + east, east), lax.rem(n + side[1] + north, north))
 
-    for side in SIDES:
-        pl.semaphore_signal(barrier, inc=1, device_id=peer(side), device_id_type=MESH)
+    for device in [peer(side) for side in SIDES] + list(others):
+        pl.semaphore_signal(barrier, inc=1, device_id=device, device_id_type=MESH)
     centre = pltpu.make_async_copy(
         x_ref, ext_ref.at[pl.ds(2, size_e), pl.ds(16, size_n * 8)], local
     )
     centre.start()
-    pl.semaphore_wait(barrier, len(SIDES))
+    pl.semaphore_wait(barrier, len(SIDES) + len(others))
     copies = [centre]
     for i, side in enumerate(SIDES):
         se, le, de = part(side[0], size_e)
@@ -135,10 +135,214 @@
         x = x_ref[pl.ds(pl.multiple_of(i * plane, 16), g_ref.shape[1])]
         y = jnp.dot(g_ref[...], x, preferred_element_type=F32)
         for b in range(9):
-            out_ref[i * 9 + b] = y[0:size, b * 128 : b * 128 + size]
+            out_ref[i * 9 + b] = y[0:size, b * 128 : (b + 1) * 128]
         return carry
 
     lax.fori_loop(0, 3, body, 0)
+
+
+class Place:
+    def __init__(self):
+        e, n = lax.axis_index("east"), lax.axis_index("north")
+        self.core = lax.rem(e, 2)
+        self.z = lax.div(e, 4)
+        self.zs = lax.axis_size("east") // 4
+        self.xs = lax.axis_size("north") // 2
+        self.x = lax.div(n, 2)
+        self.y = lax.rem(lax.div(e, 2), 2) * 2 + lax.rem(n, 2)
+
+    def device(self, core=None, x=None, y=None, z=None):
+        core = self.core if core is None else core
+        x = self.x if x is None else x
+        y = self.y if y is None else y
+        z = self.z if z is None else z
+        return (z * 4 + lax.div(y, 2) * 2 + core, x * 2 + lax.rem(y, 2))
+
+    def partner(self):
+        return self.device(core=1 - self.core)
+
+    def along(self, axis, step):
+        if axis == "x":
+            at = lax.rem(self.x + step, self.xs)
+            return at, self.device(x=at)
+        if axis == "y":
+            at = lax.rem(self.y + step, 4)
+            return at, self.device(y=at)
+        at = lax.rem(self.z + step, self.zs)
+        return at, self.device(z=at)
+
+    def peers(self):
+        found = [self.partner()]
+        for axis, count in (("x", self.xs), ("y", 4), ("z", self.zs)):
+            found += [self.along(axis, step)[1] for step in range(1, count)]
+        return found
+
+
+def all_reduce(place, src, full, got_core, held, got_one, one, held_one, got_two, slots, send, recv):
+    rows = src.shape[0]
+    half = rows // 2
+    stream = half // 2
+    wide = stream // 4
+    piece = wide // 4
+    orders = (("x", "y"), ("y", "x"))
+    here = {"x": place.x, "y": place.y}
+    started = []
+
+    def go(a, b, device):
+        i = len(started)
+        copy = pltpu.make_async_remote_copy(
+            src_ref=a, dst_ref=b, send_sem=send.at[i], recv_sem=recv.at[i],
+            device_id=device, device_id_type=MESH,
+        )
+        copy.start()
+        started.append(copy)
+        return copy
+
+    def at(start, size):
+        return pl.ds(pl.multiple_of(start, 32), size)
+
+    mine = place.core * half
+    copies = [go(src.at[at((1 - place.core) * half, half)], got_core, place.partner())]
+    yield
+
+    copies.pop().wait_recv()
+
+    def pair(i, carry):
+        total = src[at(mine + i * 128, 128)] + got_core[at(i * 128, 128)]
+        held[at(i * 128, 128)] = total.astype(BF)
+        return carry
+
+    lax.fori_loop(0, half // 128, pair, 0)
+    for s, (axis, _) in enumerate(orders):
+        for step in range(1, 4):
+            there, device = place.along(axis, step)
+            copies.append(go(held.at[at(s * stream + there * wide, wide)], got_one.at[s, step - 1], device))
+    yield
+
+    for copy in copies:
+        copy.wait_recv()
+    copies = []
+    for s, (axis, other) in enumerate(orders):
+        start = s * stream + here[axis] * wide
+        total = src[at(mine + start, wide)] + got_core[at(start, wide)]
+        for step in range(3):
+            total = total + got_one[s, step].astype(F32)
+        one[s] = total
+        held_one[s] = total.astype(BF)
+        for step in range(1, 4):
+            there, device = place.along(other, step)
+            copies.append(go(held_one.at[s, at(there * piece, piece)], got_two.at[s, step - 1], device))
+    yield
+
+    for copy in copies:
+        copy.wait_recv()
+    copies = []
+    for s, (_, other) in enumerate(orders):
+        total = one[s, at(here[other] * piece, piece)]
+        for step in range(3):
+            total = total + got_two[s, step].astype(F32)
+        slots[place.z, s * piece : (s + 1) * piece] = total.astype(BF)
+    for step in range(1, place.zs):
+        _, device = place.along("z", step)
+        copies.append(go(slots.at[place.z], slots.at[place.z], device))
+    yield
+
+    for copy in copies:
+        copy.wait_recv()
+    copies = []
+    total = slots[0].astype(F32)
+    for z in range(1, place.zs):
+        total = total + slots[z].astype(F32)
+    for s, (axis, other) in enumerate(orders):
+        rows_here = at(mine + s * stream + here[axis] * wide + here[other] * piece, piece)
+        full[rows_here] = total[s * piece : (s + 1) * piece].astype(BF)
+        for step in range(1, 4):
+            _, device = place.along(other, step)
+            copies.append(go(full.at[rows_here], full.at[rows_here], device))
+    yield
+
+    for copy in copies:
+        copy.wait_recv()
+    copies = []
+    for s, (axis, _) in enumerate(orders):
+        rows_here = at(mine + s * stream + here[axis] * wide, wide)
+        for step in range(1, 4):
+            _, device = place.along(axis, step)
+            copies.append(go(full.at[rows_here], full.at[rows_here], device))
+    yield
+
+    for copy in copies:
+        copy.wait_recv()
+    copies = [go(full.at[at(mine, half)], full.at[at(mine, half)], place.partner())]
+    yield
+
+    copies.pop().wait_recv()
+    for copy in started:
+        copy.wait_send()
+    yield
+
+
+REDUCE_COPIES = 40
+
+
+def reduce_scratch(rows, zs):
+    half = rows // 2
+    return [
+        VM((rows, 128), BF),
+        VM((half, 128), F32),
+        VM((half, 128), BF),
+        VM((2, 3, half // 8, 128), BF),
+        VM((2, half // 8, 128), F32),
+        VM((2, half // 8, 128), BF),
+        VM((2, 3, half // 32, 128), BF),
+        VM((zs, half // 16, 128), BF),
+        pltpu.SemaphoreType.DMA((REDUCE_COPIES,)),
+        pltpu.SemaphoreType.DMA((REDUCE_COPIES,)),
+    ]
+
+
+PACKED = 2048
+
+
+def pack(grad_ref, out_ref):
+    size = grad_ref.shape[1]
+    lane = lax.broadcasted_iota(jnp.int32, (size, 128), 1)
+
+    def body(g, carry):
+        spare = grad_ref[g * 4 + 3]
+        for j in range(3):
+            moved = pltpu.roll(spare, 96 - 32 * j, 1)
+            rows = pl.ds(pl.multiple_of((g * 3 + j) * size, 32), size)
+            out_ref[rows] = jnp.where(lane < 96, grad_ref[g * 4 + j], moved)
+        return carry
+
+    lax.fori_loop(0, 6, body, 0)
+    for j in range(3):
+        out_ref[(18 + j) * size : (19 + j) * size] = grad_ref[24 + j]
+    out_ref[21 * size :] = jnp.zeros((out_ref.shape[0] - 21 * size, 128), F32)
+
+
+def unpack(full_ref, out_ref, scale):
+    size = out_ref.shape[1]
+    lane = lax.broadcasted_iota(jnp.int32, (size, 128), 1)
+
+    def take(block):
+        rows = pl.ds(pl.multiple_of(block * size, 32), size)
+        return full_ref[rows].astype(F32) * scale
+
+    def body(g, carry):
+        spare = []
+        for j in range(3):
+            value = take(g * 3 + j)
+            out_ref[g * 4 + j] = value[:, 0:size]
+            spare.append(pltpu.roll(value, 32 + 32 * j, 1))
+        value = jnp.where(lane < 32, spare[0], jnp.where(lane < 64, spare[1], spare[2]))
+        out_ref[g * 4 + 3] = value[:, 0:size]
+        return carry
+
+    lax.fori_loop(0, 6, body, 0)
+    for j in range(3):
+        out_ref[24 + j] = take(18 + j)[:, 0:size]
 
 
 def slope_of(value, sig):
@@ -148,7 +352,7 @@
 def forward_kernel(
     x_ref, w1_ref, w2_ref, head_ref, teacher_ref,
     g2_ref, ext_out, slope_out, grad_ref,
-    ext_ref, wf1, wf2, cols1, cols2, acc, a1_ref, gt_ref,
+    ext_ref, wf1, wf2, cols1, cols2, acc, a1_ref, gt_ref, part_ref,
     send, recv, local,
 ):
     copies = exchange_start(x_ref, ext_ref, send, recv, local)
@@ -200,26 +404,35 @@
         return carry
 
     lax.fori_loop(0, size_e, second, 0)
-    weight_grad(gt_ref, cols2, rows, grad_ref)
+    weight_grad(gt_ref, cols2, rows, part_ref)
+    pack(part_ref, grad_ref)
 
 
 def backward_kernel(
-    g2_ref, w1_ref, w2_ref, ext0_ref, slope_ref,
-    out_ref, grad_ref,
-    ext_ref, wb1, wb2, cols0, cols1, cols2, acc, g1_ref, gt_ref,
-    send, recv, local,
+    scale, g2_ref, w1_ref, w2_ref, ext0_ref, slope_ref, packed2_ref,
+    out_ref, grad1_ref, grad2_ref,
+    ext_ref, wb1, wb2, cols0, cols1, cols2, acc, g1_ref, gt_ref, part_ref, packed1_ref,
+    send, recv, local, *rest,
 ):
-    copies = exchange_start(g2_ref, ext_ref, send, recv, local)
+    place = Place()
+    half = len(rest) // 2
+    copies = exchange_start(g2_ref, ext_ref, send, recv, local, place.peers())
+    two = all_reduce(place, packed2_ref, *rest[:half])
+    one = all_reduce(place, packed1_ref, *rest[half:])
+    next(two)
     size_e, rows = g2_ref.shape[0], g2_ref.shape[1]
     north = rows // 8
     wide = rows + 16
     channels = w1_ref.shape[1]
     lay_backward(w1_ref, wb1)
     lay_backward(w2_ref, wb2)
+    next(two)
     build(ext0_ref, 1, size_e + 2, 1, north, cols0)
     exchange_end(copies, ext_ref)
+    next(two)
     build(ext_ref, 0, size_e + 4, 0, north + 2, cols1)
     convolve(cols1, wide, (size_e + 2) * wide, wb2, acc, False)
+    next(two)
 
     def first(i, carry):
         at = pl.ds(pl.multiple_of(i * wide, 16), wide)
@@ -234,9 +447,16 @@
         return carry
 
     lax.fori_loop(0, size_e, turn, 0)
-    weight_grad(gt_ref, cols0, rows, grad_ref)
+    weight_grad(gt_ref, cols0, rows, part_ref)
+    pack(part_ref, packed1_ref)
+    next(one)
+    next(two)
     build(g1_ref, 0, size_e + 2, 0, north, cols2)
+    next(one)
+    next(two)
     convolve(cols2, rows, size_e * rows, wb1, acc, False)
+    next(one)
+    next(two)
 
     def last(i, carry):
         at = pl.ds(pl.multiple_of(i * rows, 16), rows)
@@ -246,6 +466,12 @@
         return carry
 
     lax.fori_loop(0, size_e, last, 0)
+    next(one)
+    next(two)
+    unpack(rest[0], grad2_ref, scale)
+    for _ in one:
+        pass
+    unpack(rest[half], grad1_ref, scale)
 
 
 def call(kernel, ident, outs, scratch, *args):
@@ -283,11 +509,16 @@
     sems = [pltpu.SemaphoreType.DMA((8,)), pltpu.SemaphoreType.DMA((8,)), pltpu.SemaphoreType.DMA]
     big = (east + 2) * (rows + 16)
     ext = (east + 4, rows + 32, 128)
+    packed = shape((PACKED, 128), F32)
+    part_sums = VM((27, channels, 128), F32)
     grad = shape((27, channels, channels), F32)
+    total_voxels = lax.axis_size("east") * lax.axis_size("north") * east * north * upward
+    scale = 1.0 / math.sqrt(total_voxels)
+    zs = lax.axis_size("east") // 4
     g2, ext0, slope, second_part = call(
         forward_kernel,
         1,
-        (shape((east, rows, 128), BF), shape(ext, BF), shape((big, 128), F32), grad),
+        (shape((east, rows, 128), BF), shape(ext, BF), shape((big, 128), F32), packed),
         [
             VM(ext, BF),
             VM((3, 128, 1152), BF),
@@ -297,6 +528,7 @@
             VM((big, 128), F32),
             VM((east + 2, rows + 16, 128), BF),
             VM((128, east * rows), BF),
+            part_sums,
         ]
         + sems,
         x0,
@@ -305,10 +537,10 @@
         wide_head,
         wide_teacher,
     )
-    out, first_part = call(
-        backward_kernel,
+    out, grad_first, grad_second = call(
+        functools.partial(backward_kernel, scale),
         2,
-        (shape((east, rows, channels), BF), grad),
+        (shape((east, rows, channels), BF), grad, grad),
         [
             VM(ext, BF),
             VM((3, 1152, 128), BF),
@@ -319,19 +551,20 @@
             VM((big, 128), F32),
             VM((east + 2, rows + 16, 128), BF),
             VM((128, east * rows), BF),
+            part_sums,
+            VM((PACKED, 128), F32),
         ]
-        + sems,
+        + sems
+        + reduce_scratch(PACKED, zs) * 2,
         g2,
         first_weights,
         second_weights,
         ext0,
         slope,
+        second_part,
     )
     grad_features = out.reshape(east, north, upward, channels).transpose(3, 0, 1, 2)
-    total_voxels = lax.axis_size("east") * lax.axis_size("north") * east * north * upward
-    scale = 1.0 / math.sqrt(total_voxels)
-    first_part, second_part = lax.psum((first_part, second_part), ("east", "north"))
-    return (grad_features, first_part * scale, second_part * scale)
+    return (grad_features, grad_first, grad_second)
 
 
 def solution(mesh):

time: 339 us -> 95.7 us (0.28)
  waiting for transfers between devices: 260 us -> 0 us
  Pallas kernels: 51 us -> 81.8 us
  between operations: 14.1 us -> 0.68 us
  local copies, waits for them, and re-layouts: 4.44 us -> 9.05 us
  other arithmetic: 7.43 us -> 3.69 us
    psum x1 -> x0, waiting for transfers between devices: 260 us -> none  [per_device(): lax.psum((first_part, second_part), ('east', 'north'))]
    pallas_call x2, Pallas kernels: 51 us -> 81.8 us  [call(): pl.pallas_call(kernel, out_shape=outs, in_specs=[pl.BlockSpec(memory_spac...]
    unnamed x6, local copies, waits for them, and re-layouts: 2.14 us -> 6.73 us
    mul x2 -> x0, other arithmetic: 3.74 us -> none  [per_device(): return (grad_features, first_part * scale, second_part * scale)]
  transfers between devices with their start and end apart: 1 -> 0, of which waited for: 1 -> 0; matrix products, arithmetic and copies ran while one was open for 0% -> 0% of each run, Pallas kernels for 0% -> 0%
where the time goes in v2:
time: 95.7 us; the launch traced here: 95.3 us
  Pallas kernels  81.8 us (85%)
  local copies, waits for them, and re-layouts  9.05 us (9%)
  other arithmetic  3.69 us (4%)
    pallas_call x2, Pallas kernels, call(): pl.pallas_call(kernel, out_shape=outs, in_specs=[pl.BlockSpec(memory_spac...  81.8 us
    unnamed x6, local copies, waits for them, and re-layouts  6.73 us

profile of v2, /device:TPU:1, one launch (start us, length us, event | category | flops | bytes accessed | tf_op | source)
XLA Modules:
  0.0 95.3 jit_solution(4540137411157346276)
XLA Ops:
  0.6 0.7 broadcast_in_dim.36
  1.4 0.1 broadcast_in_dim.37
  1.5 0.8 multiply_compare_fusion
  2.2 0.1 copy.11
  2.3 0.8 multiply_convert_fusion
  3.1 0.1 copy.10
  3.2 1.3 %pad.13.head_ref = bf16[128,128]{1,0:T(8,128)(2,1)} pad(bf16[13,96]{1,0:T(8,128)(2,1)} %param.12, bf16[]{:T(256)} %constant.2.clone.1), padding=0_115x0_32 | pad | bytes 35266 | tf_op jit(solution)/shard_map/jit(_pad)/pad | solution.py:507
  4.5 1.1 %select_bitcast_fusion.1 = bf16[8,16,8,96]{3,2,1,0:T(8,128)(2,1)S(1)} fusion(bf16[96,8,16,8]{0,3,2,1:T(8,128)(2,1)} %param.7, pred[8,16,8]{2,1,0:T(8,128)(4,1)S(1)} %copy.11), kind=kLoop, calls=%fused_computation.2 | loop fusion | flops 98304 | bytes 394240 | tf_op jit(solution)/shard_map/jit(_where)/select_n | solution.py:501
  5.7 1.4 %copy.13 = bf16[8,16,8,13]{3,2,1,0:T(8,128)(2,1)S(1)} copy(bf16[8,16,8,13]{1,2,0,3:T(8,128)(2,1)} %bitcast.12) | data formatting | bytes 53248
  7.1 1.0 %pad_bitcast_fusion = (bf16[8,128,128]{2,1,0:T(8,128)(2,1)}, bf16[8,128,128]{2,1,0:T(8,128)(2,1)}) fusion(bf16[8,16,8,13]{3,2,1,0:T(8,128)(2,1)S(1)} %copy.13, bf16[8,16,8,96]{3,2,1,0:T(8,128)(2,1)S(1)} %select_bitcast_fusion.1, bf16[8,16,8]{2,1,0:T(8,128)(2,1)S(1)} %copy.10, pred[128]{0:T(512)(128)(4,1)S(1)} %iota_compare_fusion), kind=kLoop, calls=%fused_computation | loop fusion | flops 131072 | bytes 749696 | tf_op jit(solution)/shard_map/reshape | solution.py:506
  8.1 30.4 %shard_map.97 = (bf16[8,128,128]{2,1,0:T(8,128)(2,1)}, bf16[12,160,128]{2,1,0:T(8,128)(2,1)}, f32[1440,128]{1,0:T(8,128)}, f32[2048,128]{1,0:T(8,128)}) custom-call(bf16[8,128,128]{2,1,0:T(8,128)(2,1)} %get-tuple-element.18.x_ref, bf16[27,96,96]{2,1,0:T(8,128)(2,1)} %w1_ref.3, bf16[27,96,96]{2,1,0:T(8,128)(2,1)} %w2_ref.3, bf16[128,128]{1,0:T(8,128)(2,1)} %pad.13.head_ref, ...), custom_call_target="tpu_custom_call" | custom-call | tf_op jit(solution)/shard_map/pallas_call | solution.py:478
  38.5 51.5 %shard_map.98 = (bf16[8,128,96]{2,1,0:T(8,128)(2,1)}, f32[27,96,96]{2,1,0:T(8,128)}, f32[27,96,96]{2,1,0:T(8,128)}) custom-call(bf16[8,128,128]{2,1,0:T(8,128)(2,1)} %get-tuple-element.10.g2_ref, bf16[27,96,96]{2,1,0:T(8,128)(2,1)} %w1_ref.3, bf16[27,96,96]{2,1,0:T(8,128)(2,1)} %w2_ref.3, bf16[12,160,128]{2,1,0:T(8,128)(2,1)} %get-tuple-element.11.ext0_ref, ...), custom_call_target="tpu_custom_call" | custom-call | tf_op jit(solution)/shard_map/pallas_call | solution.py:478
  89.9 1.7 %copy.17 = bf16[96,8,16,8]{0,3,2,1:T(8,128)(2,1)} copy(bf16[96,8,16,8]{0,3,2,1:T(8,128)(2,1)} %bitcast.11) | data formatting | bytes 393216
  91.6 0.0 copy-start
  91.6 2.6 %copy.18 = f32[27,96,96]{2,1,0:T(8,128)} copy(f32[27,96,96]{2,1,0:T(8,128)} %get-tuple-element.23) | data formatting | bytes 1990656
  94.2 0.0 copy-done
  94.2 1.1 %copy.19 = f32[27,96,96]{2,1,0:T(8,128)} copy(f32[27,96,96]{2,1,0:T(8,128)S(1)} %copy-done) | data formatting | bytes 1990656
  (1 shorter events, 0.0 us)
Async XLA Ops:
  91.6 2.6 %copy-start = (f32[27,96,96]{2,1,0:T(8,128)S(1)}, f32[27,96,96]{2,1,0:T(8,128)}, u32[]{:S(2)}) copy-start(f32[27,96,96]{2,1,0:T(8,128)} %get-tuple-element.24) | copy-start | bytes 2985988

commit v3 on v2

--- a/solution.py
+++ b/solution.py
@@ -24,32 +24,24 @@
     return 0, size, 2
 
 
-def exchange_start(x_ref, ext_ref, send, recv, local, others=()):
+def around():
     east, north = lax.axis_size("east"), lax.axis_size("north")
     e, n = lax.axis_index("east"), lax.axis_index("north")
-    size_e, size_n = x_ref.shape[0], x_ref.shape[1] // 8
-    barrier = pltpu.get_barrier_semaphore()
-
-    def peer(side):
-        return (lax.rem(e + side[0] + east, east), lax.rem(n + side[1] + north, north))
-
-    for device in [peer(side) for side in SIDES] + list(others):
-        pl.semaphore_signal(barrier, inc=1, device_id=device, device_id_type=MESH)
-    centre = pltpu.make_async_copy(
-        x_ref, ext_ref.at[pl.ds(2, size_e), pl.ds(16, size_n * 8)], local
-    )
-    centre.start()
-    pl.semaphore_wait(barrier, len(SIDES) + len(others))
-    copies = [centre]
-    for i, side in enumerate(SIDES):
+    return [(lax.rem(e + a + east, east), lax.rem(n + b + north, north)) for a, b in SIDES]
+
+
+def exchange_start(ext_ref, send, recv):
+    size_e, size_n = ext_ref.shape[0] - 4, ext_ref.shape[1] // 8 - 4
+    copies = []
+    for i, (side, device) in enumerate(zip(SIDES, around())):
         se, le, de = part(side[0], size_e)
         sn, ln, dn = part(side[1], size_n)
         copy = pltpu.make_async_remote_copy(
-            src_ref=x_ref.at[pl.ds(se, le), pl.ds(sn * 8, ln * 8)],
+            src_ref=ext_ref.at[pl.ds(se + 2, le), pl.ds((sn + 2) * 8, ln * 8)],
             dst_ref=ext_ref.at[pl.ds(de, le), pl.ds(dn * 8, ln * 8)],
             send_sem=send.at[i],
             recv_sem=recv.at[i],
-            device_id=peer(side),
+            device_id=device,
             device_id_type=MESH,
         )
         copy.start()
@@ -349,97 +341,146 @@
     return sig * (1.0 + value * (1.0 - sig))
 
 
-def forward_kernel(
-    x_ref, w1_ref, w2_ref, head_ref, teacher_ref,
-    g2_ref, ext_out, slope_out, grad_ref,
-    ext_ref, wf1, wf2, cols1, cols2, acc, a1_ref, gt_ref, part_ref,
-    send, recv, local,
+def lay_teacher(teacher_ref, flat_ref, out_ref):
+    classes, east, up, north = teacher_ref.shape
+    flat_ref[...] = teacher_ref[...].astype(F32).reshape(flat_ref.shape)
+    rows = classes * east
+    parts = [flat_ref[pl.ds(u, rows, stride=up), :] for u in range(up)]
+    wide = jnp.concatenate(parts, axis=1).astype(BF)
+    wide = jnp.concatenate([wide, jnp.zeros((128 - rows, 128), BF)], axis=0)
+    turned = lax.dot_general(reorder(up, north), wide, NT, preferred_element_type=F32)
+    out_ref[...] = turned.astype(BF)
+
+
+def reorder(up, north):
+    row = lax.broadcasted_iota(jnp.int32, (up * north, up * north), 0)
+    col = lax.broadcasted_iota(jnp.int32, (up * north, up * north), 1)
+    return jnp.where(col == (row % up) * north + row // up, 1.0, 0.0).astype(BF)
+
+
+def fill(features_ref, brick_ref, occupancy_ref, ext_ref):
+    east, up, north = occupancy_ref.shape
+    channels = features_ref.shape[2]
+    bricks = brick_ref.shape[0]
+    brick = lax.broadcasted_iota(jnp.int32, (east, north), 1) // (north // bricks)
+    flags = jnp.zeros((east, north), jnp.int32)
+    for b in range(bricks):
+        flags = jnp.where(brick == b, brick_ref[b], flags)
+    parts = [(occupancy_ref[:, u, :] * flags).astype(F32) for u in range(up)]
+    wide = jnp.concatenate(parts, axis=1).astype(BF)
+    mask = lax.dot_general(reorder(up, north), wide, NT, preferred_element_type=F32)
+    rows = up * north
+    lane = lax.broadcasted_iota(jnp.int32, (rows, 128 - channels), 1)
+    for e in range(east):
+        column = mask[:, e : e + 1]
+        x = features_ref[e].astype(F32)
+        kept = jnp.where(jnp.broadcast_to(column, x.shape) > 0, x, 0.0)
+        spare = jnp.where(lane == 0, jnp.broadcast_to(column, lane.shape), 0.0)
+        both = jnp.concatenate([kept, spare], axis=1)
+        ext_ref[e + 2, 16 : 16 + rows] = both.astype(BF)
+
+
+def main_kernel(
+    features_ref, brick_ref, occupancy_ref, w1_hbm, w2_hbm, head_ref, teacher_ref,
+    out_hbm, full1_hbm, full2_hbm,
+    ext0_ref, ext2_ref, w1_ref, w2_ref, wf1, wf2, wb1, wb2, wide_head, flat_teacher, turned,
+    cols0, cols1, cols2, acc, a1_ref, slope_ref, g1_ref, gt_ref, part_ref,
+    packed1_ref, packed2_ref, out_ref,
+    send0, recv0, send2, recv2, local, *rest,
 ):
-    copies = exchange_start(x_ref, ext_ref, send, recv, local)
-    lay_forward(w1_ref, wf1)
-    lay_forward(w2_ref, wf2)
-    exchange_end(copies, ext_ref)
-    size_e, rows = x_ref.shape[0], x_ref.shape[1]
+    place = Place()
+    devices = around() + place.peers()
+    barrier = pltpu.get_barrier_semaphore()
+    for device in devices:
+        pl.semaphore_signal(barrier, inc=1, device_id=device, device_id_type=MESH)
+    weights1 = pltpu.make_async_copy(w1_hbm, w1_ref, local.at[0])
+    weights2 = pltpu.make_async_copy(w2_hbm, w2_ref, local.at[1])
+    weights1.start()
+    weights2.start()
+    half = len(rest) // 2
+    two = all_reduce(place, packed2_ref, *rest[:half])
+    one = all_reduce(place, packed1_ref, *rest[half:])
+    size_e, rows, channels = features_ref.shape
+    classes = head_ref.shape[0]
     north = rows // 8
     wide = rows + 16
-    channels = w1_ref.shape[1]
-    ext_out[...] = ext_ref[...]
-    build(ext_ref, 0, size_e + 4, 0, north + 2, cols1)
+
+    fill(features_ref, brick_ref, occupancy_ref, ext0_ref)
+    pl.semaphore_wait(barrier, len(devices))
+    copies = exchange_start(ext0_ref, send0, recv0)
+    wide_head[...] = jnp.zeros_like(wide_head)
+    wide_head[0:classes, 0:channels] = head_ref[...]
+    lay_teacher(teacher_ref, flat_teacher, turned)
+    weights1.wait()
+    lay_forward(w1_ref, wf1)
+    lay_backward(w1_ref, wb1)
+    weights2.wait()
+    lay_forward(w2_ref, wf2)
+    lay_backward(w2_ref, wb2)
+    exchange_end(copies, ext0_ref)
+
+    build(ext0_ref, 0, size_e + 4, 0, north + 2, cols1)
     convolve(cols1, wide, (size_e + 2) * wide, wf1, acc, True)
 
     def first(i, carry):
         at = pl.ds(pl.multiple_of(i * wide, 16), wide)
-        x = ext_ref[i + 1].astype(F32)[8 : 8 + wide]
+        x = ext0_ref[i + 1].astype(F32)[8 : 8 + wide]
         mask = jnp.broadcast_to(x[:, channels : channels + 1], (wide, 128))
         p1 = mask * acc[at]
         sig = jax.nn.sigmoid(p1)
         a1_ref[i] = (p1 * sig).astype(BF)
-        slope_out[at] = mask * slope_of(p1, sig)
+        slope_ref[at] = mask * slope_of(p1, sig)
         return carry
 
     lax.fori_loop(0, size_e + 2, first, 0)
     build(a1_ref, 0, size_e + 2, 0, north, cols2)
     convolve(cols2, rows, size_e * rows, wf2, acc, True)
-    head = head_ref[...]
+    head = wide_head[...]
+    row = lax.broadcasted_iota(jnp.int32, (128, 128), 0)
+    col = lax.broadcasted_iota(jnp.int32, (128, 128), 1)
 
     def second(i, carry):
         at = pl.ds(pl.multiple_of(i * rows, 16), rows)
-        x = ext_ref[i + 2, 16 : 16 + rows].astype(F32)
+        x = ext0_ref[i + 2, 16 : 16 + rows].astype(F32)
         mask = jnp.broadcast_to(x[:, channels : channels + 1], (rows, 128))
         p2 = mask * acc[at]
         sig = jax.nn.sigmoid(p2)
         a2 = (p2 * sig).astype(BF)
         logits = lax.dot_general(a2, head, NT, preferred_element_type=F32)
-        g = mask * (logits - teacher_ref[i].astype(F32))
+        pick = jnp.where((row == col * size_e + i) & (col < classes), 1.0, 0.0).astype(BF)
+        teacher = jnp.dot(turned[...], pick, preferred_element_type=F32)
+        g = mask * (logits - teacher)
         high = g.astype(BF)
-        rest = g - high.astype(F32)
-        mid = rest.astype(BF)
-        low = (rest - mid.astype(F32)).astype(BF)
+        left = g - high.astype(F32)
+        mid = left.astype(BF)
+        low = (left - mid.astype(F32)).astype(BF)
         back = jnp.dot(low, head, preferred_element_type=F32)
         back = back + jnp.dot(mid, head, preferred_element_type=F32)
         back = back + jnp.dot(high, head, preferred_element_type=F32)
         g2 = (mask * back * slope_of(p2, sig)).astype(BF)
-        g2_ref[i] = g2
+        ext2_ref[i + 2, 16 : 16 + rows] = g2
         gt_ref[:, at] = g2.astype(F32).T.astype(BF)
         return carry
 
     lax.fori_loop(0, size_e, second, 0)
+    copies = exchange_start(ext2_ref, send2, recv2)
     weight_grad(gt_ref, cols2, rows, part_ref)
-    pack(part_ref, grad_ref)
-
-
-def backward_kernel(
-    scale, g2_ref, w1_ref, w2_ref, ext0_ref, slope_ref, packed2_ref,
-    out_ref, grad1_ref, grad2_ref,
-    ext_ref, wb1, wb2, cols0, cols1, cols2, acc, g1_ref, gt_ref, part_ref, packed1_ref,
-    send, recv, local, *rest,
-):
-    place = Place()
-    half = len(rest) // 2
-    copies = exchange_start(g2_ref, ext_ref, send, recv, local, place.peers())
-    two = all_reduce(place, packed2_ref, *rest[:half])
-    one = all_reduce(place, packed1_ref, *rest[half:])
-    next(two)
-    size_e, rows = g2_ref.shape[0], g2_ref.shape[1]
-    north = rows // 8
-    wide = rows + 16
-    channels = w1_ref.shape[1]
-    lay_backward(w1_ref, wb1)
-    lay_backward(w2_ref, wb2)
+    pack(part_ref, packed2_ref)
     next(two)
     build(ext0_ref, 1, size_e + 2, 1, north, cols0)
-    exchange_end(copies, ext_ref)
-    next(two)
-    build(ext_ref, 0, size_e + 4, 0, north + 2, cols1)
+    exchange_end(copies, ext2_ref)
+    next(two)
+    build(ext2_ref, 0, size_e + 4, 0, north + 2, cols1)
+    next(two)
     convolve(cols1, wide, (size_e + 2) * wide, wb2, acc, False)
     next(two)
 
-    def first(i, carry):
+    def third(i, carry):
         at = pl.ds(pl.multiple_of(i * wide, 16), wide)
         g1_ref[i] = (acc[at] * slope_ref[at]).astype(BF)
         return carry
 
-    lax.fori_loop(0, size_e + 2, first, 0)
+    lax.fori_loop(0, size_e + 2, third, 0)
 
     def turn(i, carry):
         at = pl.ds(pl.multiple_of(i * rows, 16), rows)
@@ -466,25 +507,25 @@
         return carry
 
     lax.fori_loop(0, size_e, last, 0)
+    saved = pltpu.make_async_copy(out_ref, out_hbm, local.at[0])
+    saved.start()
     next(one)
     next(two)
-    unpack(rest[0], grad2_ref, scale)
+    put2 = pltpu.make_async_copy(rest[0], full2_hbm, local.at[1])
+    put2.start()
     for _ in one:
         pass
-    unpack(rest[half], grad1_ref, scale)
-
-
-def call(kernel, ident, outs, scratch, *args):
-    return pl.pallas_call(
-        kernel,
-        out_shape=outs,
-        in_specs=[pl.BlockSpec(memory_space=VM)] * len(args),
-        out_specs=[pl.BlockSpec(memory_space=VM)] * len(outs),
-        scratch_shapes=scratch,
-        compiler_params=pltpu.CompilerParams(
-            collective_id=ident, has_side_effects=True, vmem_limit_bytes=60 << 20
-        ),
-    )(*args)
+    put1 = pltpu.make_async_copy(rest[half], full1_hbm, local.at[2])
+    put1.start()
+    saved.wait()
+    put2.wait()
+    put1.wait()
+
+
+def finish_kernel(scale, out_ref, full1_ref, full2_ref, grad_features_ref, grad1_ref, grad2_ref):
+    grad_features_ref[...] = out_ref[...]
+    unpack(full1_ref, grad1_ref, scale)
+    unpack(full2_ref, grad2_ref, scale)
 
 
 def per_device(
@@ -493,77 +534,62 @@
     channels, east, north, upward = features.shape
     classes = head.shape[0]
     rows = north * upward
-    flags = jnp.repeat(brick_active, east // brick_active.shape[0], 0)
-    flags = jnp.repeat(flags, north // brick_active.shape[1], 1)
-    flags = jnp.repeat(flags, upward // brick_active.shape[2], 2)
-    mask = (flags * voxel_occupancy)[..., None]
-    a0 = features.transpose(1, 2, 3, 0)
-    a0 = jnp.where(mask > 0, a0, jnp.zeros_like(a0))
-    a0 = jnp.pad(a0, ((0, 0), (0, 0), (0, 0), (0, 128 - channels)))
-    lane = lax.broadcasted_iota(jnp.int32, (1, 1, 1, 128), 3)
-    x0 = jnp.where(lane == channels, mask.astype(BF), a0).reshape(east, rows, 128)
-    wide_teacher = jnp.pad(teacher.transpose(1, 2, 3, 0), ((0, 0), (0, 0), (0, 0), (0, 128 - classes)))
-    wide_teacher = wide_teacher.reshape(east, rows, 128)
-    wide_head = jnp.pad(head, ((0, 128 - classes), (0, 128 - channels)))
     shape = jax.ShapeDtypeStruct
-    sems = [pltpu.SemaphoreType.DMA((8,)), pltpu.SemaphoreType.DMA((8,)), pltpu.SemaphoreType.DMA]
-    big = (east + 2) * (rows + 16)
-    ext = (east + 4, rows + 32, 128)
-    packed = shape((PACKED, 128), F32)
-    part_sums = VM((27, channels, 128), F32)
+    sems = pltpu.SemaphoreType.DMA
+    wide = rows + 16
+    ext = VM((east + 4, rows + 32, 128), BF)
+    field = VM((east + 2, wide, 128), BF)
+    weights = VM(first_weights.shape, BF)
+    forward, backward = VM((3, 128, 1152), BF), VM((3, 1152, 128), BF)
+    narrow_cols = VM(((east + 2) * rows, 1152), BF)
+    out = shape((east, rows, channels), BF)
+    full = shape((PACKED, 128), BF)
     grad = shape((27, channels, channels), F32)
+    vmem, anywhere = pl.BlockSpec(memory_space=VM), pl.BlockSpec(memory_space=pl.ANY)
+    packed = VM((PACKED, 128), F32)
+    result = pl.pallas_call(
+        main_kernel,
+        out_shape=(out, full, full),
+        in_specs=[vmem, pl.BlockSpec(memory_space=pltpu.SMEM), vmem, anywhere, anywhere, vmem, vmem],
+        out_specs=[anywhere] * 3,
+        scratch_shapes=[
+            ext, ext, weights, weights, forward, forward, backward, backward,
+            VM((128, 128), BF),
+            VM((classes * east * upward, north), F32),
+            VM((128, 128), BF),
+            narrow_cols, VM(((east + 4) * wide, 1152), BF), narrow_cols,
+            VM(((east + 2) * wide, 128), F32),
+            field,
+            VM(((east + 2) * wide, 128), F32),
+            field,
+            VM((128, east * rows), BF),
+            VM((27, channels, 128), F32),
+            packed, packed,
+            VM((east, rows, channels), BF),
+            sems((8,)), sems((8,)), sems((8,)), sems((8,)), sems((3,)),
+        ]
+        + reduce_scratch(PACKED, lax.axis_size("east") // 4) * 2,
+        compiler_params=pltpu.CompilerParams(
+            collective_id=1, has_side_effects=True, vmem_limit_bytes=60 << 20
+        ),
+    )(
+        features.transpose(1, 2, 3, 0).reshape(east, rows, channels),
+        brick_active.reshape(-1),
+        voxel_occupancy.transpose(0, 2, 1),
+        first_weights,
+        second_weights,
+        head,
+        teacher.transpose(0, 1, 3, 2),
+    )
     total_voxels = lax.axis_size("east") * lax.axis_size("north") * east * north * upward
     scale = 1.0 / math.sqrt(total_voxels)
-    zs = lax.axis_size("east") // 4
-    g2, ext0, slope, second_part = call(
-        forward_kernel,
-        1,
-        (shape((east, rows, 128), BF), shape(ext, BF), shape((big, 128), F32), packed),
-        [
-            VM(ext, BF),
-            VM((3, 128, 1152), BF),
-            VM((3, 128, 1152), BF),
-            VM(((east + 4) * (rows + 16), 1152), BF),
-            VM(((east + 2) * rows, 1152), BF),
-            VM((big, 128), F32),
-            VM((east + 2, rows + 16, 128), BF),
-            VM((128, east * rows), BF),
-            part_sums,
-        ]
-        + sems,
-        x0,
-        first_weights,
-        second_weights,
-        wide_head,
-        wide_teacher,
-    )
-    out, grad_first, grad_second = call(
-        functools.partial(backward_kernel, scale),
-        2,
-        (shape((east, rows, channels), BF), grad, grad),
-        [
-            VM(ext, BF),
-            VM((3, 1152, 128), BF),
-            VM((3, 1152, 128), BF),
-            VM(((east + 2) * rows, 1152), BF),
-            VM(((east + 4) * (rows + 16), 1152), BF),
-            VM(((east + 2) * rows, 1152), BF),
-            VM((big, 128), F32),
-            VM((east + 2, rows + 16, 128), BF),
-            VM((128, east * rows), BF),
-            part_sums,
-            VM((PACKED, 128), F32),
-        ]
-        + sems
-        + reduce_scratch(PACKED, zs) * 2,
-        g2,
-        first_weights,
-        second_weights,
-        ext0,
-        slope,
-        second_part,
-    )
-    grad_features = out.reshape(east, north, upward, channels).transpose(3, 0, 1, 2)
+    grad_features, grad_first, grad_second = pl.pallas_call(
+        functools.partial(finish_kernel, scale),
+        out_shape=(out, grad, grad),
+        in_specs=[vmem] * 3,
+        out_specs=[vmem] * 3,
+    )(*result)
+    grad_features = grad_features.reshape(east, north, upward, channels).transpose(3, 0, 1, 2)
     return (grad_features, grad_first, grad_second)
 
 

time: 95.7 us -> 79.4 us (0.83)
  local copies, waits for them, and re-layouts: 9.05 us -> 0 us
  other arithmetic: 3.69 us -> 0 us
  Pallas kernels: 81.8 us -> 78.7 us
    unnamed x6 -> x0, local copies, waits for them, and re-layouts: 6.73 us -> none
    pallas_call x2, Pallas kernels: 81.8 us -> 78.7 us  [the longest x1 74.6 us: per_device(): pl.pallas_call(main_kernel, out_shape=(out, full, full), in_specs=[vmem,...]
    pad x1 -> x0, local copies, waits for them, and re-layouts: 1.31 us -> none  [per_device(): wide_head = jnp.pad(head, ((0, 128 - classes), (0, 128 - channels)))]
    select_n x1 -> x0, other arithmetic: 1.15 us -> none  [per_device(): a0 = jnp.where(mask > 0, a0, jnp.zeros_like(a0))]
    reshape x1 -> x0, other arithmetic: 1 us -> none  [per_device(): wide_teacher = wide_teacher.reshape(east, rows, 128)]
where the time goes in v3:
time: 79.4 us; the launch traced here: 79.3 us
  Pallas kernels  78.7 us (99%)
    pallas_call x1, Pallas kernels, per_device(): pl.pallas_call(main_kernel, out_shape=(out, full, full), in_specs=[vmem,...  74.6 us
    pallas_call x1, Pallas kernels, per_device(): pl.pallas_call(functools.partial(finish_kernel, scale), out_shape=(out, g...  4.12 us

profile of v3, /device:TPU:1, one launch (start us, length us, event | category | flops | bytes accessed | tf_op | source)
XLA Modules:
  0.0 79.3 jit_solution(8440742108183251481)
XLA Ops:
  0.6 74.6 %shard_map.94 = (bf16[8,128,96]{2,1,0:T(8,128)(2,1)}, bf16[2048,128]{1,0:T(8,128)(2,1)}, bf16[2048,128]{1,0:T(8,128)(2,1)}) custom-call(bf16[8,128,96]{2,1,0:T(8,128)(2,1)} %bitcast.9, s32[2]{0:T(128)} %bitcast.12, s32[8,8,16]{2,1,0:T(8,128)} %bitcast.11, bf16[27,96,96]{2,1,0:T(8,128)(2,1)} %w1_hbm.1, bf16[27,96,96]{2,1,0:T(8,128)(2,1)} %w2_hbm.1, ...), custom_call_target="tpu_custom_call" | custom-call | tf_op jit(solution)/shard_map/pallas_call | solution.py:550
  75.2 4.1 %shard_map.95 = (bf16[8,128,96]{2,1,0:T(8,128)(2,1)}, f32[27,96,96]{2,1,0:T(8,128)}, f32[27,96,96]{2,1,0:T(8,128)}) custom-call(bf16[8,128,96]{2,1,0:T(8,128)(2,1)} %get-tuple-element.9.out_ref, bf16[2048,128]{1,0:T(8,128)(2,1)} %get-tuple-element.10.full1_ref, bf16[2048,128]{1,0:T(8,128)(2,1)} %get-tuple-element.11.full2_ref), custom_call_target="tpu_custom_call" | custom-call | tf_op jit(solution)/shard_map/pallas_call | solution.py:586

commit v4 on v3

--- a/solution.py
+++ b/solution.py
@@ -153,31 +153,30 @@
     def partner(self):
         return self.device(core=1 - self.core)
 
-    def along(self, axis, step):
-        if axis == "x":
-            at = lax.rem(self.x + step, self.xs)
-            return at, self.device(x=at)
-        if axis == "y":
-            at = lax.rem(self.y + step, 4)
-            return at, self.device(y=at)
-        at = lax.rem(self.z + step, self.zs)
-        return at, self.device(z=at)
+    def plane(self):
+        steps = [(a, b) for a in range(self.xs) for b in range(4) if (a, b) != (0, 0)]
+        steps.sort(key=lambda s: (min(s[0], self.xs - s[0]) + min(s[1], 4 - s[1]), s))
+        found = []
+        for a, b in steps:
+            x, y = lax.rem(self.x + a, self.xs), lax.rem(self.y + b, 4)
+            back = steps.index(((self.xs - a) % self.xs, (4 - b) % 4))
+            found.append((x * 4 + y, self.device(x=x, y=y), back))
+        return found
+
+    def column(self):
+        found = []
+        for step in range(1, self.zs):
+            found.append(self.device(z=lax.rem(self.z + step, self.zs)))
+        return found
 
     def peers(self):
-        found = [self.partner()]
-        for axis, count in (("x", self.xs), ("y", 4), ("z", self.zs)):
-            found += [self.along(axis, step)[1] for step in range(1, count)]
-        return found
-
-
-def all_reduce(place, src, full, got_core, held, got_one, one, held_one, got_two, slots, send, recv):
-    rows = src.shape[0]
-    half = rows // 2
-    stream = half // 2
-    wide = stream // 4
-    piece = wide // 4
-    orders = (("x", "y"), ("y", "x"))
-    here = {"x": place.x, "y": place.y}
+        return [self.partner()] + [device for _, device, _ in self.plane()] + self.column()
+
+
+def all_reduce(place, src, full, away, got_core, held, got, slots, send, recv):
+    half = src.shape[0] // 2
+    plane = place.plane()
+    piece = half // (len(plane) + 1)
     started = []
 
     def go(a, b, device):
@@ -191,103 +190,84 @@
         return copy
 
     def at(start, size):
-        return pl.ds(pl.multiple_of(start, 32), size)
+        return pl.ds(pl.multiple_of(start, 64), size)
 
     mine = place.core * half
-    copies = [go(src.at[at((1 - place.core) * half, half)], got_core, place.partner())]
-    yield
-
-    copies.pop().wait_recv()
-
-    def pair(i, carry):
-        total = src[at(mine + i * 128, 128)] + got_core[at(i * 128, 128)]
-        held[at(i * 128, 128)] = total.astype(BF)
-        return carry
-
-    lax.fori_loop(0, half // 128, pair, 0)
-    for s, (axis, _) in enumerate(orders):
-        for step in range(1, 4):
-            there, device = place.along(axis, step)
-            copies.append(go(held.at[at(s * stream + there * wide, wide)], got_one.at[s, step - 1], device))
+    theirs = (1 - place.core) * half
+
+    def cast(i, carry):
+        away[at(i * 256, 256)] = src[at(theirs + i * 256, 256)].astype(BF)
+        return carry
+
+    lax.fori_loop(0, half // 256, cast, 0)
+    copies = [go(away, got_core, place.partner())]
     yield
 
     for copy in copies:
         copy.wait_recv()
+
+    def pair(i, carry):
+        total = src[at(mine + i * 256, 256)] + got_core[at(i * 256, 256)].astype(F32)
+        held[at(i * 256, 256)] = total.astype(BF)
+        return carry
+
+    lax.fori_loop(0, half // 256, pair, 0)
     copies = []
-    for s, (axis, other) in enumerate(orders):
-        start = s * stream + here[axis] * wide
-        total = src[at(mine + start, wide)] + got_core[at(start, wide)]
-        for step in range(3):
-            total = total + got_one[s, step].astype(F32)
-        one[s] = total
-        held_one[s] = total.astype(BF)
-        for step in range(1, 4):
-            there, device = place.along(other, step)
-            copies.append(go(held_one.at[s, at(there * piece, piece)], got_two.at[s, step - 1], device))
+    for i, (there, device, _) in enumerate(plane):
+        copies.append(go(held.at[at(there * piece, piece)], got.at[i], device))
+    yield
+
+    own = (place.x * 4 + place.y) * piece
+    total = src[at(mine + own, piece)] + got_core[at(own, piece)].astype(F32)
+    for i, copy in enumerate(copies):
+        copy.wait_recv()
+        total = total + got[i].astype(F32)
+    slots[place.z] = total.astype(BF)
+    copies = []
+    for device in place.column():
+        copies.append(go(slots.at[place.z], slots.at[place.z], device))
     yield
 
     for copy in copies:
         copy.wait_recv()
-    copies = []
-    for s, (_, other) in enumerate(orders):
-        total = one[s, at(here[other] * piece, piece)]
-        for step in range(3):
-            total = total + got_two[s, step].astype(F32)
-        slots[place.z, s * piece : (s + 1) * piece] = total.astype(BF)
-    for step in range(1, place.zs):
-        _, device = place.along("z", step)
-        copies.append(go(slots.at[place.z], slots.at[place.z], device))
-    yield
-
-    for copy in copies:
-        copy.wait_recv()
-    copies = []
     total = slots[0].astype(F32)
     for z in range(1, place.zs):
         total = total + slots[z].astype(F32)
-    for s, (axis, other) in enumerate(orders):
-        rows_here = at(mine + s * stream + here[axis] * wide + here[other] * piece, piece)
-        full[rows_here] = total[s * piece : (s + 1) * piece].astype(BF)
-        for step in range(1, 4):
-            _, device = place.along(other, step)
-            copies.append(go(full.at[rows_here], full.at[rows_here], device))
+    rows = at(mine + own, piece)
+    full[rows] = total.astype(BF)
+    copies = []
+    for _, device, _ in plane:
+        copies.append(go(full.at[rows], full.at[rows], device))
+    last = [go(full.at[rows], full.at[rows], place.partner())]
+    yield
+
+    for copy, (_, _, back) in zip(copies, plane):
+        copy.wait_recv()
+        rows = at(mine + plane[back][0] * piece, piece)
+        last.append(go(full.at[rows], full.at[rows], place.partner()))
+    copies = last
     yield
 
     for copy in copies:
         copy.wait_recv()
-    copies = []
-    for s, (axis, _) in enumerate(orders):
-        rows_here = at(mine + s * stream + here[axis] * wide, wide)
-        for step in range(1, 4):
-            _, device = place.along(axis, step)
-            copies.append(go(full.at[rows_here], full.at[rows_here], device))
-    yield
-
-    for copy in copies:
-        copy.wait_recv()
-    copies = [go(full.at[at(mine, half)], full.at[at(mine, half)], place.partner())]
-    yield
-
-    copies.pop().wait_recv()
     for copy in started:
         copy.wait_send()
     yield
 
 
-REDUCE_COPIES = 40
-
-
-def reduce_scratch(rows, zs):
+REDUCE_COPIES = 56
+
+
+def reduce_scratch(rows, places, zs):
     half = rows // 2
+    piece = half // places
     return [
         VM((rows, 128), BF),
-        VM((half, 128), F32),
         VM((half, 128), BF),
-        VM((2, 3, half // 8, 128), BF),
-        VM((2, half // 8, 128), F32),
-        VM((2, half // 8, 128), BF),
-        VM((2, 3, half // 32, 128), BF),
-        VM((zs, half // 16, 128), BF),
+        VM((half, 128), BF),
+        VM((half, 128), BF),
+        VM((places - 1, piece, 128), BF),
+        VM((zs, piece, 128), BF),
         pltpu.SemaphoreType.DMA((REDUCE_COPIES,)),
         pltpu.SemaphoreType.DMA((REDUCE_COPIES,)),
     ]
@@ -314,15 +294,21 @@
     out_ref[21 * size :] = jnp.zeros((out_ref.shape[0] - 21 * size, 128), F32)
 
 
-def unpack(full_ref, out_ref, scale):
+def unpack(full_ref, out_ref, scale, out_hbm, sems):
     size = out_ref.shape[1]
     lane = lax.broadcasted_iota(jnp.int32, (size, 128), 1)
+    copies = []
 
     def take(block):
-        rows = pl.ds(pl.multiple_of(block * size, 32), size)
-        return full_ref[rows].astype(F32) * scale
-
-    def body(g, carry):
+        return full_ref[block * size : (block + 1) * size].astype(F32) * scale
+
+    def put(start, count):
+        part = pl.ds(start, count)
+        copy = pltpu.make_async_copy(out_ref.at[part], out_hbm.at[part], sems.at[len(copies)])
+        copy.start()
+        copies.append(copy)
+
+    for g in range(6):
         spare = []
         for j in range(3):
             value = take(g * 3 + j)
@@ -330,11 +316,11 @@
             spare.append(pltpu.roll(value, 32 + 32 * j, 1))
         value = jnp.where(lane < 32, spare[0], jnp.where(lane < 64, spare[1], spare[2]))
         out_ref[g * 4 + 3] = value[:, 0:size]
-        return carry
-
-    lax.fori_loop(0, 6, body, 0)
+        put(g * 4, 4)
     for j in range(3):
         out_ref[24 + j] = take(18 + j)[:, 0:size]
+    put(24, 3)
+    return copies
 
 
 def slope_of(value, sig):
@@ -381,11 +367,11 @@
 
 
 def main_kernel(
-    features_ref, brick_ref, occupancy_ref, w1_hbm, w2_hbm, head_ref, teacher_ref,
+    features_hbm, brick_ref, occupancy_hbm, w1_hbm, w2_hbm, head_ref, teacher_hbm,
     out_hbm, full1_hbm, full2_hbm,
     ext0_ref, ext2_ref, w1_ref, w2_ref, wf1, wf2, wb1, wb2, wide_head, flat_teacher, turned,
     cols0, cols1, cols2, acc, a1_ref, slope_ref, g1_ref, gt_ref, part_ref,
-    packed1_ref, packed2_ref, out_ref,
+    packed1_ref, packed2_ref, out_ref, features_ref, occupancy_ref, teacher_ref,
     send0, recv0, send2, recv2, local, *rest,
 ):
     place = Place()
@@ -393,10 +379,13 @@
     barrier = pltpu.get_barrier_semaphore()
     for device in devices:
         pl.semaphore_signal(barrier, inc=1, device_id=device, device_id_type=MESH)
-    weights1 = pltpu.make_async_copy(w1_hbm, w1_ref, local.at[0])
-    weights2 = pltpu.make_async_copy(w2_hbm, w2_ref, local.at[1])
-    weights1.start()
-    weights2.start()
+    pairs = (
+        (features_hbm, features_ref), (occupancy_hbm, occupancy_ref),
+        (w1_hbm, w1_ref), (w2_hbm, w2_ref), (teacher_hbm, teacher_ref),
+    )
+    loads = [pltpu.make_async_copy(a, b, local.at[3 + i]) for i, (a, b) in enumerate(pairs)]
+    for load in loads:
+        load.start()
     half = len(rest) // 2
     two = all_reduce(place, packed2_ref, *rest[:half])
     one = all_reduce(place, packed1_ref, *rest[half:])
@@ -405,16 +394,19 @@
     north = rows // 8
     wide = rows + 16
 
+    loads[0].wait()
+    loads[1].wait()
     fill(features_ref, brick_ref, occupancy_ref, ext0_ref)
     pl.semaphore_wait(barrier, len(devices))
     copies = exchange_start(ext0_ref, send0, recv0)
     wide_head[...] = jnp.zeros_like(wide_head)
     wide_head[0:classes, 0:channels] = head_ref[...]
+    loads[4].wait()
     lay_teacher(teacher_ref, flat_teacher, turned)
-    weights1.wait()
+    loads[2].wait()
     lay_forward(w1_ref, wf1)
     lay_backward(w1_ref, wb1)
-    weights2.wait()
+    loads[3].wait()
     lay_forward(w2_ref, wf2)
     lay_backward(w2_ref, wb2)
     exchange_end(copies, ext0_ref)
@@ -439,17 +431,23 @@
     row = lax.broadcasted_iota(jnp.int32, (128, 128), 0)
     col = lax.broadcasted_iota(jnp.int32, (128, 128), 1)
 
+    group = 4
+
     def second(i, carry):
-        at = pl.ds(pl.multiple_of(i * rows, 16), rows)
-        x = ext0_ref[i + 2, 16 : 16 + rows].astype(F32)
-        mask = jnp.broadcast_to(x[:, channels : channels + 1], (rows, 128))
+        planes = pl.ds(i * group + 2, group)
+        at = pl.ds(pl.multiple_of(i * (group * rows), 128), group * rows)
+        x = ext0_ref[planes, 16 : 16 + rows].astype(F32).reshape(group * rows, 128)
+        mask = jnp.broadcast_to(x[:, channels : channels + 1], (group * rows, 128))
         p2 = mask * acc[at]
         sig = jax.nn.sigmoid(p2)
         a2 = (p2 * sig).astype(BF)
         logits = lax.dot_general(a2, head, NT, preferred_element_type=F32)
-        pick = jnp.where((row == col * size_e + i) & (col < classes), 1.0, 0.0).astype(BF)
-        teacher = jnp.dot(turned[...], pick, preferred_element_type=F32)
-        g = mask * (logits - teacher)
+        teacher = []
+        for b in range(group):
+            pick = (row == col * size_e + (i * group + b)) & (col < classes)
+            pick = jnp.where(pick, 1.0, 0.0).astype(BF)
+            teacher.append(jnp.dot(turned[...], pick, preferred_element_type=F32))
+        g = mask * (logits - jnp.concatenate(teacher, axis=0))
         high = g.astype(BF)
         left = g - high.astype(F32)
         mid = left.astype(BF)
@@ -458,20 +456,19 @@
         back = back + jnp.dot(mid, head, preferred_element_type=F32)
         back = back + jnp.dot(high, head, preferred_element_type=F32)
         g2 = (mask * back * slope_of(p2, sig)).astype(BF)
-        ext2_ref[i + 2, 16 : 16 + rows] = g2
+        ext2_ref[planes, 16 : 16 + rows] = g2.reshape(group, rows, 128)
         gt_ref[:, at] = g2.astype(F32).T.astype(BF)
         return carry
 
-    lax.fori_loop(0, size_e, second, 0)
+    lax.fori_loop(0, size_e // group, second, 0)
     copies = exchange_start(ext2_ref, send2, recv2)
     weight_grad(gt_ref, cols2, rows, part_ref)
     pack(part_ref, packed2_ref)
     next(two)
     build(ext0_ref, 1, size_e + 2, 1, north, cols0)
+    next(two)
     exchange_end(copies, ext2_ref)
-    next(two)
     build(ext2_ref, 0, size_e + 4, 0, north + 2, cols1)
-    next(two)
     convolve(cols1, wide, (size_e + 2) * wide, wb2, acc, False)
     next(two)
 
@@ -491,13 +488,10 @@
     weight_grad(gt_ref, cols0, rows, part_ref)
     pack(part_ref, packed1_ref)
     next(one)
-    next(two)
     build(g1_ref, 0, size_e + 2, 0, north, cols2)
     next(one)
     next(two)
     convolve(cols2, rows, size_e * rows, wb1, acc, False)
-    next(one)
-    next(two)
 
     def last(i, carry):
         at = pl.ds(pl.multiple_of(i * rows, 16), rows)
@@ -511,10 +505,12 @@
     saved.start()
     next(one)
     next(two)
+    next(one)
+    next(two)
     put2 = pltpu.make_async_copy(rest[0], full2_hbm, local.at[1])
     put2.start()
-    for _ in one:
-        pass
+    next(one)
+    next(one)
     put1 = pltpu.make_async_copy(rest[half], full1_hbm, local.at[2])
     put1.start()
     saved.wait()
@@ -522,10 +518,23 @@
     put1.wait()
 
 
-def finish_kernel(scale, out_ref, full1_ref, full2_ref, grad_features_ref, grad1_ref, grad2_ref):
-    grad_features_ref[...] = out_ref[...]
-    unpack(full1_ref, grad1_ref, scale)
-    unpack(full2_ref, grad2_ref, scale)
+def finish_kernel(
+    scale, out_in, full1_in, full2_in, out_hbm, grad1_hbm, grad2_hbm,
+    out_ref, full1_ref, full2_ref, grad1_ref, grad2_ref, loads, stores1, stores2,
+):
+    pairs = ((full2_in, full2_ref), (full1_in, full1_ref), (out_in, out_ref))
+    copies = [pltpu.make_async_copy(a, b, loads.at[i]) for i, (a, b) in enumerate(pairs)]
+    for copy in copies:
+        copy.start()
+    copies[0].wait()
+    stores = unpack(full2_ref, grad2_ref, scale, grad2_hbm, stores2)
+    copies[1].wait()
+    stores += unpack(full1_ref, grad1_ref, scale, grad1_hbm, stores1)
+    copies[2].wait()
+    saved = pltpu.make_async_copy(out_ref, out_hbm, loads.at[3])
+    saved.start()
+    for copy in stores + [saved]:
+        copy.wait()
 
 
 def per_device(
@@ -550,7 +559,7 @@
     result = pl.pallas_call(
         main_kernel,
         out_shape=(out, full, full),
-        in_specs=[vmem, pl.BlockSpec(memory_space=pltpu.SMEM), vmem, anywhere, anywhere, vmem, vmem],
+        in_specs=[anywhere, pl.BlockSpec(memory_space=pltpu.SMEM), anywhere, anywhere, anywhere, vmem, anywhere],
         out_specs=[anywhere] * 3,
         scratch_shapes=[
             ext, ext, weights, weights, forward, forward, backward, backward,
@@ -566,9 +575,12 @@
             VM((27, channels, 128), F32),
             packed, packed,
             VM((east, rows, channels), BF),
-            sems((8,)), sems((8,)), sems((8,)), sems((8,)), sems((3,)),
+            VM((east, rows, channels), BF),
+            VM((east, upward, north), jnp.int32),
+            VM(head.shape[:1] + (east, upward, north), BF),
+            sems((8,)), sems((8,)), sems((8,)), sems((8,)), sems((8,)),
         ]
-        + reduce_scratch(PACKED, lax.axis_size("east") // 4) * 2,
+        + reduce_scratch(PACKED, lax.axis_size("north") * 2, lax.axis_size("east") // 4) * 2,
         compiler_params=pltpu.CompilerParams(
             collective_id=1, has_side_effects=True, vmem_limit_bytes=60 << 20
         ),
@@ -586,8 +598,11 @@
     grad_features, grad_first, grad_second = pl.pallas_call(
         functools.partial(finish_kernel, scale),
         out_shape=(out, grad, grad),
-        in_specs=[vmem] * 3,
-        out_specs=[vmem] * 3,
+        in_specs=[anywhere] * 3,
+        out_specs=[anywhere] * 3,
+        scratch_shapes=[VM(a.shape, a.dtype) for a in (out, full, full, grad, grad)]
+        + [sems((4,)), sems((7,)), sems((7,))],
+        compiler_params=pltpu.CompilerParams(vmem_limit_bytes=60 << 20),
     )(*result)
     grad_features = grad_features.reshape(east, north, upward, channels).transpose(3, 0, 1, 2)
     return (grad_features, grad_first, grad_second)

time: 79.4 us -> 67.5 us (0.85)
  Pallas kernels: 78.7 us -> 66.7 us
    pallas_call x1, Pallas kernels: 74.6 us -> 63.8 us  [per_device(): pl.pallas_call(main_kernel, out_shape=(out, full, full), in_specs=[anywhe...]
    pallas_call x1, Pallas kernels: 4.12 us -> 2.88 us  [per_device(): pl.pallas_call(functools.partial(finish_kernel, scale), out_shape=(out, g...]
where the time goes in v4:
time: 67.5 us; the launch traced here: 67.3 us
  Pallas kernels  66.7 us (99%)
    pallas_call x1, Pallas kernels, per_device(): pl.pallas_call(main_kernel, out_shape=(out, full, full), in_specs=[anywhe...  63.8 us
    pallas_call x1, Pallas kernels, per_device(): pl.pallas_call(functools.partial(finish_kernel, scale), out_shape=(out, g...  2.88 us

profile of v4, /device:TPU:1, one launch (start us, length us, event | category | flops | bytes accessed | tf_op | source)
XLA Modules:
  0.0 67.3 jit_solution(1514105643474310185)
XLA Ops:
  0.6 63.8 %shard_map.94 = (bf16[8,128,96]{2,1,0:T(8,128)(2,1)}, bf16[2048,128]{1,0:T(8,128)(2,1)}, bf16[2048,128]{1,0:T(8,128)(2,1)}) custom-call(bf16[8,128,96]{2,1,0:T(8,128)(2,1)} %bitcast.9, s32[2]{0:T(128)} %bitcast.12, s32[8,8,16]{2,1,0:T(8,128)} %bitcast.11, bf16[27,96,96]{2,1,0:T(8,128)(2,1)} %w1_hbm.1, bf16[27,96,96]{2,1,0:T(8,128)(2,1)} %w2_hbm.1, ...), custom_call_target="tpu_custom_call" | custom-call | tf_op jit(solution)/shard_map/pallas_call | solution.py:559
  64.4 2.9 %shard_map.95 = (bf16[8,128,96]{2,1,0:T(8,128)(2,1)}, f32[27,96,96]{2,1,0:T(8,128)}, f32[27,96,96]{2,1,0:T(8,128)}) custom-call(bf16[8,128,96]{2,1,0:T(8,128)(2,1)} %get-tuple-element.9.out_in, bf16[2048,128]{1,0:T(8,128)(2,1)} %get-tuple-element.10.full1_in, bf16[2048,128]{1,0:T(8,128)(2,1)} %get-tuple-element.11.full2_in), custom_call_target="tpu_custom_call" | custom-call | tf_op jit(solution)/shard_map/pallas_call | solution.py:598

commit v5 on v4

--- a/solution.py
+++ b/solution.py
@@ -12,7 +12,7 @@
 VM = pltpu.VMEM
 F32 = jnp.float32
 BF = jnp.bfloat16
-SIDES = tuple((a, b) for a in (-1, 0, 1) for b in (-1, 0, 1) if (a, b) != (0, 0))
+SIDES = ((-1, -1), (-1, 1), (1, -1), (1, 1), (-1, 0), (1, 0), (0, -1), (0, 1))
 NT = (((1,), (1,)), ((), ()))
 
 
@@ -30,14 +30,14 @@
     return [(lax.rem(e + a + east, east), lax.rem(n + b + north, north)) for a, b in SIDES]
 
 
-def exchange_start(ext_ref, send, recv):
+def exchange_start(x_ref, ext_ref, send, recv):
     size_e, size_n = ext_ref.shape[0] - 4, ext_ref.shape[1] // 8 - 4
     copies = []
     for i, (side, device) in enumerate(zip(SIDES, around())):
         se, le, de = part(side[0], size_e)
         sn, ln, dn = part(side[1], size_n)
         copy = pltpu.make_async_remote_copy(
-            src_ref=ext_ref.at[pl.ds(se + 2, le), pl.ds((sn + 2) * 8, ln * 8)],
+            src_ref=x_ref.at[pl.ds(se + 2, le), pl.ds((sn + 2) * 8, ln * 8)],
             dst_ref=ext_ref.at[pl.ds(de, le), pl.ds(dn * 8, ln * 8)],
             send_sem=send.at[i],
             recv_sem=recv.at[i],
@@ -105,22 +105,65 @@
         out_ref[k // 9, (k % 9) * 128 : (k % 9) * 128 + size, 0:size] = w_ref[26 - k]
 
 
+def product(x, w, transposed):
+    if transposed:
+        return lax.dot_general(x, w, NT, preferred_element_type=F32)
+    return jnp.dot(x, w, preferred_element_type=F32)
+
+
 def convolve(x_ref, plane, rows, w_ref, acc_ref, transposed):
-    acc_ref[0:rows] = jnp.zeros((rows, 128), F32)
+    total = product(x_ref[0:rows], w_ref[0], transposed)
+    for i in (1, 2):
+        total = total + product(x_ref[i * plane : i * plane + rows], w_ref[i], transposed)
+    acc_ref[0:rows] = total
+
+
+def build_halo(ext_ref, out_ref):
+    planes, rows = ext_ref.shape[0], ext_ref.shape[1] - 16
+    inner = planes - 4
+    build(ext_ref, 0, 2, 0, rows // 8, out_ref.at[0 : 2 * rows])
+    build(ext_ref, planes - 2, 2, 0, rows // 8, out_ref.at[2 * rows + 32 * inner :])
+    wide = ext_ref.shape[1] // 8
+    up = lax.broadcasted_iota(jnp.int32, (4, 8, 128), 1)
+    zero = jnp.zeros((2, 8, 128), F32)
 
     def body(i, carry):
-        x = x_ref[pl.ds(pl.multiple_of(i * plane, 16), rows)]
-        if transposed:
-            y = lax.dot_general(x, w_ref[i], NT, preferred_element_type=F32)
-        else:
-            y = jnp.dot(x, w_ref[i], preferred_element_type=F32)
-        acc_ref[0:rows] += y
-        return carry
-
-    lax.fori_loop(0, 3, body, 0)
-
-
-def weight_grad(g_ref, x_ref, plane, out_ref):
+        x = ext_ref[i + 2].astype(F32).reshape(wide, 8, 128)
+        x = jnp.concatenate([x[0:2], x[wide - 2 :]], axis=0)
+        below = jnp.where(up == 0, 0.0, pltpu.roll(x, 1, 1))
+        above = jnp.where(up == 7, 0.0, pltpu.roll(x, 7, 1))
+        at = pl.ds(pl.multiple_of(2 * rows + i * 32, 16), 32)
+        for dn in range(3):
+            for du, piece in enumerate((below, x, above)):
+                block = (dn * 3 + du) * 128
+                low = jnp.concatenate([piece[0:2], zero], axis=0)[dn : dn + 2]
+                high = jnp.concatenate([zero, piece[2:4]], axis=0)[dn : dn + 2]
+                y = jnp.concatenate([low, high], axis=0).reshape(32, 128)
+                out_ref[at, block : block + 128] = y.astype(BF)
+        return carry
+
+    lax.fori_loop(0, inner, body, 0)
+
+
+def convolve_halo(x_ref, plane, inner, w_ref, acc_ref, transposed):
+    count = 2 * plane + 32 * inner
+    last = inner + 1
+    for i in range(3):
+        y = product(x_ref[i * plane : i * plane + count], w_ref[i], transposed)
+        before = (2 - i) * plane
+        if before:
+            acc_ref[0:before] += y[0:before]
+        if i:
+            start = (last + 1 - i) * plane
+            acc_ref[start : start + i * plane] += y[count - i * plane :]
+        for e in range(inner):
+            at = (e + 2 - i) * plane
+            part = before + e * 32
+            acc_ref[at : at + 16] += y[part : part + 16]
+            acc_ref[at + plane - 16 : at + plane] += y[part + 16 : part + 32]
+
+
+def weight_grad(g_ref, x_ref, plane, out_ref, begin=0, end=3):
     size = out_ref.shape[1]
 
     def body(i, carry):
@@ -190,7 +233,7 @@
         return copy
 
     def at(start, size):
-        return pl.ds(pl.multiple_of(start, 64), size)
+        return pl.ds(pl.multiple_of(start, 32), size)
 
     mine = place.core * half
     theirs = (1 - place.core) * half
@@ -276,7 +319,7 @@
 PACKED = 2048
 
 
-def pack(grad_ref, out_ref):
+def pack(grad_ref, out_ref, begin=0, end=6):
     size = grad_ref.shape[1]
     lane = lax.broadcasted_iota(jnp.int32, (size, 128), 1)
 
@@ -288,7 +331,9 @@
             out_ref[rows] = jnp.where(lane < 96, grad_ref[g * 4 + j], moved)
         return carry
 
-    lax.fori_loop(0, 6, body, 0)
+    lax.fori_loop(begin, end, body, 0)
+    if end < 6:
+        return
     for j in range(3):
         out_ref[(18 + j) * size : (19 + j) * size] = grad_ref[24 + j]
     out_ref[21 * size :] = jnp.zeros((out_ref.shape[0] - 21 * size, 128), F32)
@@ -344,7 +389,7 @@
     return jnp.where(col == (row % up) * north + row // up, 1.0, 0.0).astype(BF)
 
 
-def fill(features_ref, brick_ref, occupancy_ref, ext_ref):
+def fill(features_ref, brick_ref, occupancy_ref, ext_ref, own_ref):
     east, up, north = occupancy_ref.shape
     channels = features_ref.shape[2]
     bricks = brick_ref.shape[0]
@@ -364,12 +409,13 @@
         spare = jnp.where(lane == 0, jnp.broadcast_to(column, lane.shape), 0.0)
         both = jnp.concatenate([kept, spare], axis=1)
         ext_ref[e + 2, 16 : 16 + rows] = both.astype(BF)
+        own_ref[e + 2, 16 : 16 + rows] = both.astype(BF)
 
 
 def main_kernel(
     features_hbm, brick_ref, occupancy_hbm, w1_hbm, w2_hbm, head_ref, teacher_hbm,
     out_hbm, full1_hbm, full2_hbm,
-    ext0_ref, ext2_ref, w1_ref, w2_ref, wf1, wf2, wb1, wb2, wide_head, flat_teacher, turned,
+    ext0_ref, own_ref, halo_cols, ext2_ref, w1_ref, w2_ref, wf1, wf2, wb1, wb2, wide_head, flat_teacher, turned,
     cols0, cols1, cols2, acc, a1_ref, slope_ref, g1_ref, gt_ref, part_ref,
     packed1_ref, packed2_ref, out_ref, features_ref, occupancy_ref, teacher_ref,
     send0, recv0, send2, recv2, local, *rest,
@@ -386,9 +432,10 @@
     loads = [pltpu.make_async_copy(a, b, local.at[3 + i]) for i, (a, b) in enumerate(pairs)]
     for load in loads:
         load.start()
-    half = len(rest) // 2
-    two = all_reduce(place, packed2_ref, *rest[:half])
-    one = all_reduce(place, packed1_ref, *rest[half:])
+    split = packed1_ref.shape[0] // 2
+    two = all_reduce(place, packed2_ref, *rest[:8])
+    one_a = all_reduce(place, packed1_ref.at[0:split], *rest[8:16])
+    one_b = all_reduce(place, packed1_ref.at[split:], *rest[16:24])
     size_e, rows, channels = features_ref.shape
     classes = head_ref.shape[0]
     north = rows // 8
@@ -396,23 +443,27 @@
 
     loads[0].wait()
     loads[1].wait()
-    fill(features_ref, brick_ref, occupancy_ref, ext0_ref)
+    fill(features_ref, brick_ref, occupancy_ref, ext0_ref, own_ref)
     pl.semaphore_wait(barrier, len(devices))
-    copies = exchange_start(ext0_ref, send0, recv0)
+    copies = exchange_start(own_ref, ext0_ref, send0, recv0)
+    edge = jnp.zeros((size_e + 4, 16, 128), BF)
+    own_ref[:, 0:16] = edge
+    own_ref[:, 16 + rows : 32 + rows] = edge
+    cols1[0 : 2 * wide] = jnp.zeros((2 * wide, cols1.shape[1]), BF)
+    cols1[(size_e + 2) * wide :] = jnp.zeros((2 * wide, cols1.shape[1]), BF)
+    build(own_ref, 2, size_e, 0, north + 2, cols1.at[2 * wide : (size_e + 2) * wide])
+    loads[2].wait()
+    lay_forward(w1_ref, wf1)
+    convolve(cols1, wide, (size_e + 2) * wide, wf1, acc, True)
+    loads[3].wait()
+    lay_forward(w2_ref, wf2)
     wide_head[...] = jnp.zeros_like(wide_head)
     wide_head[0:classes, 0:channels] = head_ref[...]
     loads[4].wait()
     lay_teacher(teacher_ref, flat_teacher, turned)
-    loads[2].wait()
-    lay_forward(w1_ref, wf1)
-    lay_backward(w1_ref, wb1)
-    loads[3].wait()
-    lay_forward(w2_ref, wf2)
-    lay_backward(w2_ref, wb2)
     exchange_end(copies, ext0_ref)
-
-    build(ext0_ref, 0, size_e + 4, 0, north + 2, cols1)
-    convolve(cols1, wide, (size_e + 2) * wide, wf1, acc, True)
+    build_halo(ext0_ref, halo_cols)
+    convolve_halo(halo_cols, wide, size_e, wf1, acc, True)
 
     def first(i, carry):
         at = pl.ds(pl.multiple_of(i * wide, 16), wide)
@@ -461,10 +512,12 @@
         return carry
 
     lax.fori_loop(0, size_e // group, second, 0)
-    copies = exchange_start(ext2_ref, send2, recv2)
+    copies = exchange_start(ext2_ref, ext2_ref, send2, recv2)
     weight_grad(gt_ref, cols2, rows, part_ref)
     pack(part_ref, packed2_ref)
     next(two)
+    lay_backward(w2_ref, wb2)
+    lay_backward(w1_ref, wb1)
     build(ext0_ref, 1, size_e + 2, 1, north, cols0)
     next(two)
     exchange_end(copies, ext2_ref)
@@ -485,11 +538,15 @@
         return carry
 
     lax.fori_loop(0, size_e, turn, 0)
-    weight_grad(gt_ref, cols0, rows, part_ref)
-    pack(part_ref, packed1_ref)
-    next(one)
+    weight_grad(gt_ref, cols0, rows, part_ref, 0, 2)
+    pack(part_ref, packed1_ref, 0, 4)
+    next(one_a)
+    weight_grad(gt_ref, cols0, rows, part_ref, 2, 3)
+    pack(part_ref, packed1_ref, 4, 6)
+    next(one_b)
+    next(one_a)
+    next(one_b)
     build(g1_ref, 0, size_e + 2, 0, north, cols2)
-    next(one)
     next(two)
     convolve(cols2, rows, size_e * rows, wb1, acc, False)
 
@@ -503,19 +560,26 @@
     lax.fori_loop(0, size_e, last, 0)
     saved = pltpu.make_async_copy(out_ref, out_hbm, local.at[0])
     saved.start()
-    next(one)
+    next(one_a)
+    next(one_b)
     next(two)
-    next(one)
+    next(one_a)
+    next(one_b)
     next(two)
     put2 = pltpu.make_async_copy(rest[0], full2_hbm, local.at[1])
     put2.start()
-    next(one)
-    next(one)
-    put1 = pltpu.make_async_copy(rest[half], full1_hbm, local.at[2])
-    put1.start()
+    next(one_a)
+    next(one_b)
+    next(one_a)
+    put1a = pltpu.make_async_copy(rest[8], full1_hbm.at[0:split], local.at[2])
+    put1a.start()
+    next(one_b)
+    put1b = pltpu.make_async_copy(rest[16], full1_hbm.at[pl.ds(split, split)], local.at[3])
+    put1b.start()
     saved.wait()
     put2.wait()
-    put1.wait()
+    put1a.wait()
+    put1b.wait()
 
 
 def finish_kernel(
@@ -562,7 +626,7 @@
         in_specs=[anywhere, pl.BlockSpec(memory_space=pltpu.SMEM), anywhere, anywhere, anywhere, vmem, anywhere],
         out_specs=[anywhere] * 3,
         scratch_shapes=[
-            ext, ext, weights, weights, forward, forward, backward, backward,
+            ext, ext, VM((4 * wide + 32 * east, 1152), BF), ext, weights, weights, forward, forward, backward, backward,
             VM((128, 128), BF),
             VM((classes * east * upward, north), F32),
             VM((128, 128), BF),
@@ -580,7 +644,11 @@
             VM(head.shape[:1] + (east, upward, north), BF),
             sems((8,)), sems((8,)), sems((8,)), sems((8,)), sems((8,)),
         ]
-        + reduce_scratch(PACKED, lax.axis_size("north") * 2, lax.axis_size("east") // 4) * 2,
+        + [
+            item
+            for size in (PACKED, PACKED // 2, PACKED // 2)
+            for item in reduce_scratch(size, lax.axis_size("north") * 2, lax.axis_size("east") // 4)
+        ],
         compiler_params=pltpu.CompilerParams(
             collective_id=1, has_side_effects=True, vmem_limit_bytes=60 << 20
         ),

time: 67.5 us -> 65.2 us (0.966)
  Pallas kernels: 66.7 us -> 64.3 us
    pallas_call x1, Pallas kernels: 63.8 us -> 61.4 us  [per_device(): pl.pallas_call(main_kernel, out_shape=(out, full, full), in_specs=[anywhe...]
where the time goes in v5:
time: 65.2 us; the launch traced here: 65.1 us
  Pallas kernels  64.3 us (99%)
  between operations  0.8 us (1%)
    pallas_call x1, Pallas kernels, per_device(): pl.pallas_call(main_kernel, out_shape=(out, full, full), in_specs=[anywhe...  61.4 us
    pallas_call x1, Pallas kernels, per_device(): pl.pallas_call(functools.partial(finish_kernel, scale), out_shape=(out, g...  2.88 us

profile of v5, /device:TPU:1, one launch (start us, length us, event | category | flops | bytes accessed | tf_op | source)
XLA Modules:
  0.0 65.1 jit_solution(6025670144866088288)
XLA Ops:
  0.6 61.4 %shard_map.94 = (bf16[8,128,96]{2,1,0:T(8,128)(2,1)}, bf16[2048,128]{1,0:T(8,128)(2,1)}, bf16[2048,128]{1,0:T(8,128)(2,1)}) custom-call(bf16[8,128,96]{2,1,0:T(8,128)(2,1)} %bitcast.9, s32[2]{0:T(128)} %bitcast.12, s32[8,8,16]{2,1,0:T(8,128)} %bitcast.11, bf16[27,96,96]{2,1,0:T(8,128)(2,1)} %w1_hbm.1, bf16[27,96,96]{2,1,0:T(8,128)(2,1)} %w2_hbm.1, ...), custom_call_target="tpu_custom_call" | custom-call | tf_op jit(solution)/shard_map/pallas_call | solution.py:623
  62.0 2.9 %shard_map.95 = (bf16[8,128,96]{2,1,0:T(8,128)(2,1)}, f32[27,96,96]{2,1,0:T(8,128)}, f32[27,96,96]{2,1,0:T(8,128)}) custom-call(bf16[8,128,96]{2,1,0:T(8,128)(2,1)} %get-tuple-element.9.out_in, bf16[2048,128]{1,0:T(8,128)(2,1)} %get-tuple-element.10.full1_in, bf16[2048,128]{1,0:T(8,128)(2,1)} %get-tuple-element.11.full2_in), custom_call_target="tpu_custom_call" | custom-call | tf_op jit(solution)/shard_map/pallas_call | solution.py:666

commit v6 on v5

--- a/solution.py
+++ b/solution.py
@@ -76,19 +76,21 @@
     wide = src_ref.shape[1] // 8
     up = lax.broadcasted_iota(jnp.int32, (wide, 8, 128), 1)
 
-    def body(i, carry):
-        x = src_ref[first + i].astype(F32).reshape(wide, 8, 128)
-        below = jnp.where(up == 0, 0.0, pltpu.roll(x, 1, 1))
-        above = jnp.where(up == 7, 0.0, pltpu.roll(x, 7, 1))
-        rows = pl.ds(pl.multiple_of(i * (count * 8), 16), count * 8)
-        for dn in range(3):
-            for du, piece in enumerate((below, x, above)):
-                block = (dn * 3 + du) * 128
-                y = piece[start + dn : start + dn + count].reshape(count * 8, 128)
-                out_ref[rows, block : block + 128] = y.astype(BF)
-        return carry
-
-    lax.fori_loop(0, planes, body, 0)
+    def body(pair, carry):
+        for half in range(2):
+            i = pair * 2 + half
+            x = src_ref[first + i].astype(F32).reshape(wide, 8, 128)
+            below = jnp.where(up == 0, 0.0, pltpu.roll(x, 1, 1))
+            above = jnp.where(up == 7, 0.0, pltpu.roll(x, 7, 1))
+            rows = pl.ds(pl.multiple_of(i * (count * 8), 16), count * 8)
+            for dn in range(3):
+                for du, piece in enumerate((below, x, above)):
+                    block = (dn * 3 + du) * 128
+                    y = piece[start + dn : start + dn + count].reshape(count * 8, 128)
+                    out_ref[rows, block : block + 128] = y.astype(BF)
+        return carry
+
+    lax.fori_loop(0, planes // 2, body, 0)
 
 
 def lay_forward(w_ref, out_ref):
@@ -465,24 +467,26 @@
     build_halo(ext0_ref, halo_cols)
     convolve_halo(halo_cols, wide, size_e, wf1, acc, True)
 
-    def first(i, carry):
-        at = pl.ds(pl.multiple_of(i * wide, 16), wide)
-        x = ext0_ref[i + 1].astype(F32)[8 : 8 + wide]
-        mask = jnp.broadcast_to(x[:, channels : channels + 1], (wide, 128))
-        p1 = mask * acc[at]
-        sig = jax.nn.sigmoid(p1)
-        a1_ref[i] = (p1 * sig).astype(BF)
-        slope_ref[at] = mask * slope_of(p1, sig)
-        return carry
-
-    lax.fori_loop(0, size_e + 2, first, 0)
+    def first(pair, carry):
+        for half in range(2):
+            i = pair * 2 + half
+            at = pl.ds(pl.multiple_of(i * wide, 16), wide)
+            x = ext0_ref[i + 1].astype(F32)[8 : 8 + wide]
+            mask = jnp.broadcast_to(x[:, channels : channels + 1], (wide, 128))
+            p1 = mask * acc[at]
+            sig = jax.nn.sigmoid(p1)
+            a1_ref[i] = (p1 * sig).astype(BF)
+            slope_ref[at] = mask * slope_of(p1, sig)
+        return carry
+
+    lax.fori_loop(0, (size_e + 2) // 2, first, 0)
     build(a1_ref, 0, size_e + 2, 0, north, cols2)
     convolve(cols2, rows, size_e * rows, wf2, acc, True)
     head = wide_head[...]
     row = lax.broadcasted_iota(jnp.int32, (128, 128), 0)
     col = lax.broadcasted_iota(jnp.int32, (128, 128), 1)
 
-    group = 4
+    group = size_e
 
     def second(i, carry):
         planes = pl.ds(i * group + 2, group)
@@ -525,19 +529,11 @@
     convolve(cols1, wide, (size_e + 2) * wide, wb2, acc, False)
     next(two)
 
-    def third(i, carry):
-        at = pl.ds(pl.multiple_of(i * wide, 16), wide)
-        g1_ref[i] = (acc[at] * slope_ref[at]).astype(BF)
-        return carry
-
-    lax.fori_loop(0, size_e + 2, third, 0)
-
-    def turn(i, carry):
-        at = pl.ds(pl.multiple_of(i * rows, 16), rows)
-        gt_ref[:, at] = g1_ref[i + 1].astype(F32)[8 : 8 + rows].T.astype(BF)
-        return carry
-
-    lax.fori_loop(0, size_e, turn, 0)
+    for i in range(size_e + 2):
+        g1 = (acc[i * wide : (i + 1) * wide] * slope_ref[i * wide : (i + 1) * wide]).astype(BF)
+        g1_ref[i] = g1
+        if 0 < i <= size_e:
+            gt_ref[:, (i - 1) * rows : i * rows] = g1.astype(F32)[8 : 8 + rows].T.astype(BF)
     weight_grad(gt_ref, cols0, rows, part_ref, 0, 2)
     pack(part_ref, packed1_ref, 0, 4)
     next(one_a)

time: 65.2 us -> 63.9 us (0.980)
  Pallas kernels: 64.3 us -> 62.9 us
    pallas_call x1, Pallas kernels: 61.4 us -> 60 us  [per_device(): pl.pallas_call(main_kernel, out_shape=(out, full, full), in_specs=[anywhe...]
where the time goes in v6:
time: 63.9 us; the launch traced here: 63.7 us
  Pallas kernels  62.9 us (98%)
  between operations  0.8 us (1%)
    pallas_call x1, Pallas kernels, per_device(): pl.pallas_call(main_kernel, out_shape=(out, full, full), in_specs=[anywhe...  60 us
    pallas_call x1, Pallas kernels, per_device(): pl.pallas_call(functools.partial(finish_kernel, scale), out_shape=(out, g...  2.88 us

profile of v6, /device:TPU:1, one launch (start us, length us, event | category | flops | bytes accessed | tf_op | source)
XLA Modules:
  0.0 63.7 jit_solution(3811367828438270341)
XLA Ops:
  0.6 60.0 %shard_map.94 = (bf16[8,128,96]{2,1,0:T(8,128)(2,1)}, bf16[2048,128]{1,0:T(8,128)(2,1)}, bf16[2048,128]{1,0:T(8,128)(2,1)}) custom-call(bf16[8,128,96]{2,1,0:T(8,128)(2,1)} %bitcast.9, s32[2]{0:T(128)} %bitcast.12, s32[8,8,16]{2,1,0:T(8,128)} %bitcast.11, bf16[27,96,96]{2,1,0:T(8,128)(2,1)} %w1_hbm.1, bf16[27,96,96]{2,1,0:T(8,128)(2,1)} %w2_hbm.1, ...), custom_call_target="tpu_custom_call" | custom-call | tf_op jit(solution)/shard_map/pallas_call | solution.py:619
  60.7 2.9 %shard_map.95 = (bf16[8,128,96]{2,1,0:T(8,128)(2,1)}, f32[27,96,96]{2,1,0:T(8,128)}, f32[27,96,96]{2,1,0:T(8,128)}) custom-call(bf16[8,128,96]{2,1,0:T(8,128)(2,1)} %get-tuple-element.9.out_in, bf16[2048,128]{1,0:T(8,128)(2,1)} %get-tuple-element.10.full1_in, bf16[2048,128]{1,0:T(8,128)(2,1)} %get-tuple-element.11.full2_in), custom_call_target="tpu_custom_call" | custom-call | tf_op jit(solution)/shard_map/pallas_call | solution.py:662

commit v7 on v6

--- a/solution.py
+++ b/solution.py
@@ -521,7 +521,6 @@
     pack(part_ref, packed2_ref)
     next(two)
     lay_backward(w2_ref, wb2)
-    lay_backward(w1_ref, wb1)
     build(ext0_ref, 1, size_e + 2, 1, north, cols0)
     next(two)
     exchange_end(copies, ext2_ref)
@@ -542,6 +541,7 @@
     next(one_b)
     next(one_a)
     next(one_b)
+    lay_backward(w1_ref, wb1)
     build(g1_ref, 0, size_e + 2, 0, north, cols2)
     next(two)
     convolve(cols2, rows, size_e * rows, wb1, acc, False)

time: 63.9 us -> 63.6 us (level)
  no operation moved by 1% of the time
where the time goes in v7:
time: 63.6 us; the launch traced here: 63.5 us
  Pallas kernels  62.7 us (99%)
  between operations  0.8 us (1%)
    pallas_call x1, Pallas kernels, per_device(): pl.pallas_call(main_kernel, out_shape=(out, full, full), in_specs=[anywhe...  59.8 us
    pallas_call x1, Pallas kernels, per_device(): pl.pallas_call(functools.partial(finish_kernel, scale), out_shape=(out, g...  2.88 us

profile of v7, /device:TPU:1, one launch (start us, length us, event | category | flops | bytes accessed | tf_op | source)
XLA Modules:
  0.0 63.5 jit_solution(4571119837595997416)
XLA Ops:
  0.6 59.8 %shard_map.94 = (bf16[8,128,96]{2,1,0:T(8,128)(2,1)}, bf16[2048,128]{1,0:T(8,128)(2,1)}, bf16[2048,128]{1,0:T(8,128)(2,1)}) custom-call(bf16[8,128,96]{2,1,0:T(8,128)(2,1)} %bitcast.9, s32[2]{0:T(128)} %bitcast.12, s32[8,8,16]{2,1,0:T(8,128)} %bitcast.11, bf16[27,96,96]{2,1,0:T(8,128)(2,1)} %w1_hbm.1, bf16[27,96,96]{2,1,0:T(8,128)(2,1)} %w2_hbm.1, ...), custom_call_target="tpu_custom_call" | custom-call | tf_op jit(solution)/shard_map/pallas_call | solution.py:619
  60.4 2.9 %shard_map.95 = (bf16[8,128,96]{2,1,0:T(8,128)(2,1)}, f32[27,96,96]{2,1,0:T(8,128)}, f32[27,96,96]{2,1,0:T(8,128)}) custom-call(bf16[8,128,96]{2,1,0:T(8,128)(2,1)} %get-tuple-element.9.out_in, bf16[2048,128]{1,0:T(8,128)(2,1)} %get-tuple-element.10.full1_in, bf16[2048,128]{1,0:T(8,128)(2,1)} %get-tuple-element.11.full2_in), custom_call_target="tpu_custom_call" | custom-call | tf_op jit(solution)/shard_map/pallas_call | solution.py:662
